TPU v7x, 32 devices: a whole 2x2x4 slice. The times are simulated.
32 devices in a mesh: groups: 2 (over x), pts: 8 (over z, y), sn: 2 (over core).
Axes of the slice: x: 2, y: 2, z: 4, core: 2. Of those that a mesh axis runs over, the one named last changes fastest.
Arguments:
- point_features: bfloat16 [131072, 192], P(('groups', 'pts', 'sn')), parts along dimension 0, may hold values from -6 to 6
- point_positions: float32 [3, 131072], P(None, ('groups', 'pts', 'sn')), parts along dimension 1, may hold values from 0 to 1
- sn_positions: float32 [3, 32768], P(None, ('groups', 'pts', 'sn')), parts along dimension 1, may hold values from 0 to 1
- latent_queries: bfloat16 [512, 192], replicated, may hold values from -500 to 500
- target_block: int32 [256], P('groups'), parts along dimension 0, may hold values from 0 to 127, as said below
- target_links: int32 [256, 3], P(('groups', 'pts', 'sn')), parts along dimension 0, may hold values from 0 to 31
- target_count: int32 [32], P('groups'), parts along dimension 0, may hold values from 6 to 8, as said below
- block_slot: int32 [256], P('groups'), parts along dimension 0, may hold values from 0 to 127, as said below
- w_in: bfloat16 [192, 192], replicated, may hold values from -0.4375 to 0.4375
- w_mid: bfloat16 [192, 192], replicated, may hold values from -0.4375 to 0.4375
- w_post: bfloat16 [192, 192], replicated, may hold values from -1.25 to 1.25
- w_key: bfloat16 [192, 192], replicated, may hold values from -0.4375 to 0.4375
- w_value: bfloat16 [192, 192], replicated, may hold values from -0.4375 to 0.4375
- w_out: bfloat16 [192, 192], replicated, may hold values from -0.4375 to 0.4375
- out_gain: float32 [192], replicated, may hold values from 0.1 to 1.9
Outputs:
- supernode_features: bfloat16 [32768, 192], P(('groups', 'pts', 'sn')), parts along dimension 0
- latent_out: bfloat16 [1024, 192], P(('groups', 'pts', 'sn')), parts along dimension 0
There are 2 independent parts, one for each index of `groups`. A program takes and returns all parts, laid end to end along the dimension named above; an argument that names none is the same for every part. Nothing has to cross between parts.
Inputs may be any that keep to these rules, and one draw needn't show every extreme that they name: `target_block`: the 8 targets of one region name blocks of distinct owners, the owner of a block being its slot divided by 8; one owner, the same for all regions, holds the first target of every region. `target_count`: the live targets of a region are its first ones; some region has all 8 live. `block_slot`: A permutation.
All inputs are finite; a program needn't handle non-finite values.
Results may differ from a plain program's by a relative error of at most 0.012.
The roundings to bfloat16 on the way count: a program that leaves them out, or rounds other values in their place, can miss the bound.
Values may be sent and summed in bfloat16 or wider, within the bound.
A program may use at most 256 MiB of HBM per device.

v0:
```python
import jax
import jax.numpy as jnp
from jax import lax
from jax.sharding import PartitionSpec as P

HEADS = 3
BLOCK = 128
KEY_BLOCK = 512
TGT_BATCH = 4


INV_RADIUS_SQ = 100.0


def merged_2(part, axis, combine):
    gathered = jax.tree.map(lambda a: lax.all_gather(a, axis), part)

    def take(source):
        return jax.tree.map(lambda a: lax.dynamic_index_in_dim(a, source, 0, False), gathered)

    return lax.fori_loop(
        1, lax.axis_size(axis), lambda source, state: combine(state, take(source)), take(0)
    )


def combine_parts(first, second):
    peak_a, total_a, output_a = first
    peak_b, total_b, output_b = second
    peak = jnp.maximum(peak_a, peak_b)
    scale_a = jnp.exp(peak_a - peak)
    scale_b = jnp.exp(peak_b - peak)
    total = total_a * scale_a + total_b * scale_b
    rows = output_a.shape[0]
    heads = peak.shape[-1]
    output = (
        output_a.reshape(rows, heads, -1) * scale_a[..., None]
        + output_b.reshape(rows, heads, -1) * scale_b[..., None]
    )
    return (peak, total, output.reshape(rows, -1))


def block_attend(queries, keys_blk, values_blk):
    rows, width = queries.shape
    head_width = width // HEADS
    query_heads = queries.reshape(rows, HEADS, head_width)
    key_heads = keys_blk.reshape(-1, HEADS, head_width)
    value_heads = values_blk.reshape(-1, HEADS, head_width)
    scores = jnp.einsum(
        "lhd,khd->lhk", query_heads, key_heads, preferred_element_type=jnp.float32
    ) * head_width ** (-0.5)
    peak = jnp.max(scores, axis=-1)
    weights = jnp.exp(scores - peak[..., None])
    total = jnp.sum(weights, axis=-1)
    output = jnp.einsum(
        "lhk,khd->lhd",
        weights.astype(jnp.bfloat16),
        value_heads,
        preferred_element_type=jnp.float32,
    )
    return (peak, total, output.reshape(rows, width))


def per_device(
    point_features,
    point_positions,
    sn_positions,
    latent_queries,
    target_block,
    target_links,
    target_count,
    block_slot,
    w_in,
    w_mid,
    w_post,
    w_key,
    w_value,
    w_out,
    out_gain,
):
    owners = lax.axis_size(("pts", "sn"))
    my_index = lax.axis_index(("pts", "sn"))
    targets = target_links.shape[0]
    links = target_links.shape[1]
    width = point_features.shape[1]
    sn_rows = sn_positions.shape[1]
    sn_blocks = sn_rows // BLOCK
    inner_act = jax.nn.gelu(
        jnp.dot(point_features, w_in, preferred_element_type=jnp.float32)
    ).astype(jnp.bfloat16)
    hidden = jnp.dot(inner_act, w_mid, preferred_element_type=jnp.float32).astype(jnp.bfloat16)
    hidden_blocks = hidden.reshape(-1, BLOCK, width)
    point_blocks = point_positions.reshape(3, -1, BLOCK)
    slot_table = block_slot[target_block].reshape(owners, targets)
    my_slots = lax.dynamic_index_in_dim(slot_table, my_index, 0, keepdims=False)
    my_count = lax.dynamic_index_in_dim(target_count, my_index, 0, keepdims=False)
    is_live = jnp.arange(targets) < my_count
    owner_of = my_slots // sn_blocks
    everywhere = lax.all_gather(sn_positions, ("pts", "sn"), axis=1, tiled=True)
    target_pos = jnp.transpose(everywhere.reshape(3, -1, BLOCK)[:, my_slots], (1, 0, 2))

    def one_batch(batch_inputs):
        link_ids, batch_pos = batch_inputs
        feats = hidden_blocks[link_ids]
        linked_pos = point_blocks[:, link_ids]
        gaps = (
            jnp.transpose(batch_pos, (1, 0, 2))[:, :, None, :, None] - linked_pos[:, :, :, None, :]
        )
        kernel = 1.0 / (1.0 + jnp.sum(gaps * gaps, axis=0) * INV_RADIUS_SQ)
        totals = jnp.sum(kernel, axis=(1, 3))
        sums = jnp.einsum(
            "tlji,tlic->tjc", kernel.astype(jnp.bfloat16), feats, preferred_element_type=jnp.float32
        )
        return (sums, totals)

    partials, totals = lax.map(
        one_batch,
        (target_links.reshape(-1, TGT_BATCH, links), target_pos.reshape(-1, TGT_BATCH, 3, BLOCK)),
    )
    partials = jnp.where(
        is_live[:, None, None], partials.reshape(targets, BLOCK, width), 0.0
    ).astype(jnp.bfloat16)
    totals = jnp.where(is_live[:, None], totals.reshape(targets, BLOCK), 0.0).astype(jnp.bfloat16)
    outgoing = jnp.zeros((owners, BLOCK, width), jnp.bfloat16).at[owner_of].set(partials)
    outgoing_tot = jnp.zeros((owners, BLOCK), jnp.bfloat16).at[owner_of].set(totals)
    arrived, arrived_tot = (
        lax.all_to_all(outgoing, ("pts", "sn"), split_axis=0, concat_axis=0, tiled=True),
        lax.all_to_all(outgoing_tot, ("pts", "sn"), split_axis=0, concat_axis=0, tiled=True),
    )
    source_live = jnp.arange(targets)[None, :] < target_count[:, None]
    to_me = (slot_table // sn_blocks == my_index) & source_live
    which_block = jnp.where(to_me, slot_table % sn_blocks, -1)
    placer = jnp.sum(
        (which_block[:, :, None] == jnp.arange(sn_blocks)[None, None, :]).astype(jnp.float32),
        axis=1,
    ).astype(jnp.bfloat16)
    gathered = jnp.einsum("sb,sjc->bjc", placer, arrived, preferred_element_type=jnp.float32)
    weight_sum = jnp.einsum("sb,sj->bj", placer, arrived_tot, preferred_element_type=jnp.float32)
    pooled = (gathered / (1.0 + weight_sum[..., None])).astype(jnp.bfloat16).reshape(sn_rows, width)
    supernode_features = jax.nn.gelu(
        jnp.dot(pooled, w_post, preferred_element_type=jnp.float32)
    ).astype(jnp.bfloat16)
    keys = jnp.dot(supernode_features, w_key, preferred_element_type=jnp.float32).astype(
        jnp.bfloat16
    )
    values = jnp.dot(supernode_features, w_value, preferred_element_type=jnp.float32).astype(
        jnp.bfloat16
    )
    rows = latent_queries.shape[0]
    init = (
        jnp.full((rows, HEADS), -jnp.inf, jnp.float32),
        jnp.zeros((rows, HEADS), jnp.float32),
        jnp.zeros((rows, width), jnp.float32),
    )

    def key_step(carry, block_inputs):
        return (
            combine_parts(carry, block_attend(latent_queries, block_inputs[0], block_inputs[1])),
            None,
        )

    partial_state, unused = lax.scan(
        key_step, init, (keys.reshape(-1, KEY_BLOCK, width), values.reshape(-1, KEY_BLOCK, width))
    )
    share = rows // owners
    merged = merged_2(partial_state, ("pts", "sn"), combine_parts)
    total = lax.dynamic_slice_in_dim(merged[1], my_index * share, share, 0)
    output = lax.dynamic_slice_in_dim(merged[2], my_index * share, share, 0)
    attended = (
        (output.reshape(share, HEADS, -1) / total[..., None])
        .reshape(share, width)
        .astype(jnp.bfloat16)
    )
    projected = jnp.dot(attended, w_out, preferred_element_type=jnp.float32)
    mean_sq = jnp.mean(projected * projected, axis=-1, keepdims=True)
    latent_out = (projected * lax.rsqrt(mean_sq + 1e-06) * out_gain).astype(jnp.bfloat16)
    return (supernode_features, latent_out)


def solution(mesh):
    in_specs = (
        P(("groups", "pts", "sn"), None),
        P(None, ("groups", "pts", "sn")),
        P(None, ("groups", "pts", "sn")),
        P(),
        P("groups"),
        P(("groups", "pts", "sn"), None),
        P("groups"),
        P("groups"),
        P(),
        P(),
        P(),
        P(),
        P(),
        P(),
        P(),
    )
    out_specs = (P(("groups", "pts", "sn"), None), P(("groups", "pts", "sn"), None))
    return jax.shard_map(
        per_device, mesh=mesh, in_specs=in_specs, out_specs=out_specs, check_vma=False
    )
```

profile of v0, /device:TPU:0, one launch (start us, length us, event | category | flops | bytes accessed | tf_op | source)
XLA Modules:
  0.0 222.8 jit_solution(13857639724945199308)
XLA Ops:
  7.2 0.8 compare_select_fusion.2
  8.0 1.6 gather_fusion.2
  9.7 0.6 fusion.68
  10.3 24.1 %all_gather.21 = f32[3,16384]{1,0:T(4,128)S(1)} all-gather(f32[3,1024]{1,0:T(4,128)} %param.23), channel_id=1, replica_groups=mesh['groups'=2,'pts'=8,'sn'=2] {'pts','sn'}, dimensions={1}, use_global_device_ids=true | all-gather | bytes 208896 | tf_op jit(solution)/shard_map/all_gather | solution.py:98
  34.4 0.6 gather_fusion.3
  35.0 2.6 %convolution_convert_fusion = bf16[4096,192]{0,1:T(8,128)(2,1)S(1)} fusion(bf16[192,192]{1,0:T(8,128)(2,1)} %param.30, bf16[4096,192]{0,1:T(8,128)(2,1)S(1)} %copy-done, bf16[192,192]{1,0:T(8,128)(2,1)} %param.29), kind=kOutput, calls=%fused_computation.48 | convolution fusion | flops 611844096 | bytes 3293184 | tf_op jit(solution)/shard_map/dot_general | solution.py:90
  37.6 2.5 %copy.93 = bf16[4096,192]{1,0:T(8,128)(2,1)} copy(bf16[4096,192]{0,1:T(8,128)(2,1)S(1)} %convolution_convert_fusion) | data formatting | bytes 3145728 | tf_op jit(solution)/shard_map/while | solution.py:115
  40.0 0.7 reshape.320
  40.7 12.1 %while.46 = (s32[]{:T(128)}, bf16[2,4,128,192]{2,3,1,0:T(8,128)(2,1)S(1)}, f32[2,4,128]{2,1,0:T(4,128)}, f32[2,4,3,128]{3,1,2,0:T(4,128)S(1)}, s32[2,4,3]{1,0,2:...) while((s32[]{:T(128)}, bf16[2,4,128,192]{2,3,1,0:T(8,128)(2,1)S(1)}, ...), condition=%wide.region_4.5_spmd, body=%wide.region_1.4_spmd.sunk | while | flops 78643752 | bytes 4840465 | solution.py:115
  40.7 0.7 compare_select_fusion.8
  41.6 1.4 gather_fusion.1
  43.3 2.2 gather_fusion
  45.5 0.5 fusion.106
  46.2 0.6 bitcast_dynamic-update-slice_fusion.2
  46.8 0.7 compare_select_fusion.8
  47.7 1.4 gather_fusion.1
  49.4 2.2 gather_fusion
  51.6 0.5 fusion.106
  52.3 0.6 bitcast_dynamic-update-slice_fusion.2
  52.8 1.4 dynamic_slice.71
  54.2 0.6 iota_compare_fusion.2
  54.8 0.8 scatter_custom_fusion.1
  55.7 0.6 copy.82
  56.3 3.5 %all-to-all-start.1 = ((bf16[16,1,128]{2,1,0:T(2,128)(2,1)}), bf16[16,1,128]{2,1,0:T(2,128)(2,1)S(1)}, u32[]{:S(2)}, u32[]{:S(2)}) async-start(bf16[16,1,128]{2,1,0:T(2,128)(2,1)} %copy.82), calls=%async_computation.1 | async-start | bytes 16384 | tf_op jit(solution)/shard_map/all_to_all | solution.py:127
  59.9 1.0 broadcast_in_dim.85
  60.9 2.6 %scatter_fusion = bf16[16,128,192]{1,2,0:T(8,128)(2,1)} fusion(bf16[16,128,192]{1,2,0:T(8,128)(2,1)} %broadcast_in_dim.85, s32[8]{0:T(128)} %get-tuple-element.447, bf16[8,128,192]{1,2,0:T(8,128)(2,1)S(1)} %fusion.45), kind=kCustom, calls=%fused_computation.4 | custom fusion | bytes 1179680 | tf_op jit(solution)/shard_map/scatter | solution.py:123
  63.5 2.5 %all-to-all-done.1 = bf16[16,1,128]{2,1,0:T(2,128)(2,1)S(1)} async-done(((bf16[16,1,128]{2,1,0:T(2,128)(2,1)}), bf16[16,1,128]{2,1,0:T(2,128)(2,1)S(1)}, u32[]{:S(2)}, u32[]{:S(2)}) %all-to-all-start.1) | async-done | bytes 4128 | tf_op jit(solution)/shard_map/all_to_all | solution.py:127
  66.1 3.6 %all-to-all-start = ((bf16[16,128,192]{1,2,0:T(8,128)(2,1)}), bf16[16,128,192]{1,2,0:T(8,128)(2,1)S(1)}, u32[]{:S(2)}, u32[]{:S(2)}) async-start(bf16[16,128,192]{1,2,0:T(8,128)(2,1)} %scatter_fusion), calls=%async_computation | async-start | bytes 1572864 | tf_op jit(solution)/shard_map/all_to_all | solution.py:126
  70.1 18.3 %all-to-all-done = bf16[16,128,192]{1,2,0:T(8,128)(2,1)S(1)} async-done(((bf16[16,128,192]{1,2,0:T(8,128)(2,1)}), bf16[16,128,192]{1,2,0:T(8,128)(2,1)S(1)}, u32[]{:S(2)}, u32[]{:S(2)}) %all-to-all-start) | async-done | bytes 786464 | tf_op jit(solution)/shard_map/all_to_all | solution.py:126
  88.3 0.5 fusion.36
  88.9 0.5 fusion.44
  89.7 0.3 convolution_convert_fusion.1
  90.1 11.1 %while.48 = (s32[]{:T(128)}, f32[512,3]{0,1:T(4,128)S(1)}, f32[512,3]{0,1:T(4,128)S(1)}, f32[512,192]{0,1:T(8,128)S(1)}, bf16[2,512,192]{1,2,0:T(8,128)(2,1)S(1)...) while((s32[]{:T(128)}, f32[512,3]{0,1:T(4,128)S(1)}, ...), condition=%wide.region_10.11_spmd.clone, body=%wide.region_7.10_spmd.clone.sunk | while | flops 207922176 | bytes 24268936 | solution.py:161
  90.2 0.6 bitcast_reduce_fusion.2
  90.8 1.6 copy-done.1
  92.5 0.5 fusion.114
  93.0 2.6 %fusion.116 = f32[512,3,64]{0,2,1:T(8,128)S(1)} fusion(bf16[512,3,64]{0,2,1:T(8,128)(2,1)S(1)} %bitcast.179, f32[3,512,512]{2,1,0:T(8,128)} %copy-done.1, f32[512,3]{0,1:T(4,128)S(1)} %get-tuple-element.599, f32[512,3,64]{0,2,1:T(8,128)S(1)} %bitcast.182, f32[512,3]{0,1:T(4,128)S(1)} %get-tuple-element.603, f32[512,3]{0,1:T(4,128)S(1)} %get-tuple-element.604), kind=kOutput, calls=%fused_computation.39.clone.1 | convolution fusion | flops 103317504 | bytes 4147200 | tf_op jit(solution)/shard_map/while/body/eval_jaxpr/lhk,khd->lhd/dot_general | solution.py:54
  95.7 0.6 bitcast_reduce_fusion.2
  96.4 1.6 copy-done.1
  98.0 0.5 fusion.114
  98.6 2.6 %fusion.116 = f32[512,3,64]{0,2,1:T(8,128)S(1)} fusion(bf16[512,3,64]{0,2,1:T(8,128)(2,1)S(1)} %bitcast.179, f32[3,512,512]{2,1,0:T(8,128)} %copy-done.1, f32[512,3]{0,1:T(4,128)S(1)} %get-tuple-element.599, f32[512,3,64]{0,2,1:T(8,128)S(1)} %bitcast.182, f32[512,3]{0,1:T(4,128)S(1)} %get-tuple-element.603, f32[512,3]{0,1:T(4,128)S(1)} %get-tuple-element.604), kind=kOutput, calls=%fused_computation.39.clone.1 | convolution fusion | flops 103317504 | bytes 4147200 | tf_op jit(solution)/shard_map/while/body/eval_jaxpr/lhk,khd->lhd/dot_general | solution.py:54
  101.2 0.7 copy-done.2
  102.0 22.1 %all-gather = f32[8192,3]{0,1:T(4,128)S(1)} all-gather(f32[512,3]{0,1:T(4,128)S(1)} %get-tuple-element.258), channel_id=2, replica_groups=mesh['groups'=2,'pts'=8,'sn'=2] {'pts','sn'}, dimensions={0}, use_global_device_ids=true | all-gather | bytes 104448 | tf_op jit(solution)/shard_map/all_gather | solution.py:16
  124.1 18.6 %all-gather.1 = f32[8192,3]{0,1:T(4,128)S(1)} all-gather(f32[512,3]{0,1:T(4,128)S(1)} %get-tuple-element.259), channel_id=3, replica_groups=mesh['groups'=2,'pts'=8,'sn'=2] {'pts','sn'}, dimensions={0}, use_global_device_ids=true | all-gather | bytes 104448 | tf_op jit(solution)/shard_map/all_gather | solution.py:16
  142.7 22.1 %all-gather.5.cloned.1.call-done = f32[8192,192]{0,1:T(8,128)} async-done(((f32[512,192]{0,1:T(8,128)}), f32[8192,192]{0,1:T(8,128)}) %all-gather.5.cloned.1.call-update) | async-done | bytes 6291472 | tf_op jit(solution)/shard_map/all_gather | solution.py:16
  164.8 10.9 %copy.99 = f32[24,8,16,512]{3,2,1,0:T(8,128)} copy(f32[24,8,16,512]{3,1,2,0:T(8,128)} %bitcast.186) | data formatting | bytes 12582912
  175.6 1.0 slice.16
  176.7 37.7 %while.47 = (s32[]{:T(128)}, f32[512,3]{0,1:T(4,128)S(1)}, f32[512,3]{0,1:T(4,128)S(1)}, f32[512,192]{0,1:T(8,128)S(1)}, f32[16,512,3]{1,2,0:T(4,128)S(1)}, /*in...) while((s32[]{:T(128)}, f32[512,3]{0,1:T(4,128)S(1)}, ...), condition=%wide.region_12.13_spmd, body=%wide.region_11.12_spmd.sunk | while | flops 304133 | bytes 2027671 | solution.py:21
  176.7 2.3 %constant_dynamic-slice_fusion.7 = f32[1,512,192]{1,0,2:T(1,128)S(1)} fusion(f32[16,512,192]{1,0,2:T(8,128)} %get-tuple-element.682, s32[]{:T(128)S(6)} %select_n.149), kind=kLoop, calls=%fused_computation.16.clone.1 | loop fusion | bytes 786436 | tf_op jit(solution)/shard_map/while/body/eval_jaxpr/jit(dynamic_index_in_dim)/dynamic_slice | solution.py:19
  179.3 2.3 %constant_dynamic-slice_fusion.7 = f32[1,512,192]{1,0,2:T(1,128)S(1)} fusion(f32[16,512,192]{1,0,2:T(8,128)} %get-tuple-element.682, s32[]{:T(128)S(6)} %select_n.149), kind=kLoop, calls=%fused_computation.16.clone.1 | loop fusion | bytes 786436 | tf_op jit(solution)/shard_map/while/body/eval_jaxpr/jit(dynamic_index_in_dim)/dynamic_slice | solution.py:19
  181.8 2.3 %constant_dynamic-slice_fusion.7 = f32[1,512,192]{1,0,2:T(1,128)S(1)} fusion(f32[16,512,192]{1,0,2:T(8,128)} %get-tuple-element.682, s32[]{:T(128)S(6)} %select_n.149), kind=kLoop, calls=%fused_computation.16.clone.1 | loop fusion | bytes 786436 | tf_op jit(solution)/shard_map/while/body/eval_jaxpr/jit(dynamic_index_in_dim)/dynamic_slice | solution.py:19
  184.3 2.3 %constant_dynamic-slice_fusion.7 = f32[1,512,192]{1,0,2:T(1,128)S(1)} fusion(f32[16,512,192]{1,0,2:T(8,128)} %get-tuple-element.682, s32[]{:T(128)S(6)} %select_n.149), kind=kLoop, calls=%fused_computation.16.clone.1 | loop fusion | bytes 786436 | tf_op jit(solution)/shard_map/while/body/eval_jaxpr/jit(dynamic_index_in_dim)/dynamic_slice | solution.py:19
  186.8 2.3 %constant_dynamic-slice_fusion.7 = f32[1,512,192]{1,0,2:T(1,128)S(1)} fusion(f32[16,512,192]{1,0,2:T(8,128)} %get-tuple-element.682, s32[]{:T(128)S(6)} %select_n.149), kind=kLoop, calls=%fused_computation.16.clone.1 | loop fusion | bytes 786436 | tf_op jit(solution)/shard_map/while/body/eval_jaxpr/jit(dynamic_index_in_dim)/dynamic_slice | solution.py:19
  189.3 2.3 %constant_dynamic-slice_fusion.7 = f32[1,512,192]{1,0,2:T(1,128)S(1)} fusion(f32[16,512,192]{1,0,2:T(8,128)} %get-tuple-element.682, s32[]{:T(128)S(6)} %select_n.149), kind=kLoop, calls=%fused_computation.16.clone.1 | loop fusion | bytes 786436 | tf_op jit(solution)/shard_map/while/body/eval_jaxpr/jit(dynamic_index_in_dim)/dynamic_slice | solution.py:19
  191.8 2.3 %constant_dynamic-slice_fusion.7 = f32[1,512,192]{1,0,2:T(1,128)S(1)} fusion(f32[16,512,192]{1,0,2:T(8,128)} %get-tuple-element.682, s32[]{:T(128)S(6)} %select_n.149), kind=kLoop, calls=%fused_computation.16.clone.1 | loop fusion | bytes 786436 | tf_op jit(solution)/shard_map/while/body/eval_jaxpr/jit(dynamic_index_in_dim)/dynamic_slice | solution.py:19
  194.3 2.3 %constant_dynamic-slice_fusion.7 = f32[1,512,192]{1,0,2:T(1,128)S(1)} fusion(f32[16,512,192]{1,0,2:T(8,128)} %get-tuple-element.682, s32[]{:T(128)S(6)} %select_n.149), kind=kLoop, calls=%fused_computation.16.clone.1 | loop fusion | bytes 786436 | tf_op jit(solution)/shard_map/while/body/eval_jaxpr/jit(dynamic_index_in_dim)/dynamic_slice | solution.py:19
  196.8 2.3 %constant_dynamic-slice_fusion.7 = f32[1,512,192]{1,0,2:T(1,128)S(1)} fusion(f32[16,512,192]{1,0,2:T(8,128)} %get-tuple-element.682, s32[]{:T(128)S(6)} %select_n.149), kind=kLoop, calls=%fused_computation.16.clone.1 | loop fusion | bytes 786436 | tf_op jit(solution)/shard_map/while/body/eval_jaxpr/jit(dynamic_index_in_dim)/dynamic_slice | solution.py:19
  199.4 2.3 %constant_dynamic-slice_fusion.7 = f32[1,512,192]{1,0,2:T(1,128)S(1)} fusion(f32[16,512,192]{1,0,2:T(8,128)} %get-tuple-element.682, s32[]{:T(128)S(6)} %select_n.149), kind=kLoop, calls=%fused_computation.16.clone.1 | loop fusion | bytes 786436 | tf_op jit(solution)/shard_map/while/body/eval_jaxpr/jit(dynamic_index_in_dim)/dynamic_slice | solution.py:19
  201.9 2.3 %constant_dynamic-slice_fusion.7 = f32[1,512,192]{1,0,2:T(1,128)S(1)} fusion(f32[16,512,192]{1,0,2:T(8,128)} %get-tuple-element.682, s32[]{:T(128)S(6)} %select_n.149), kind=kLoop, calls=%fused_computation.16.clone.1 | loop fusion | bytes 786436 | tf_op jit(solution)/shard_map/while/body/eval_jaxpr/jit(dynamic_index_in_dim)/dynamic_slice | solution.py:19
  204.4 2.3 %constant_dynamic-slice_fusion.7 = f32[1,512,192]{1,0,2:T(1,128)S(1)} fusion(f32[16,512,192]{1,0,2:T(8,128)} %get-tuple-element.682, s32[]{:T(128)S(6)} %select_n.149), kind=kLoop, calls=%fused_computation.16.clone.1 | loop fusion | bytes 786436 | tf_op jit(solution)/shard_map/while/body/eval_jaxpr/jit(dynamic_index_in_dim)/dynamic_slice | solution.py:19
  206.9 2.3 %constant_dynamic-slice_fusion.7 = f32[1,512,192]{1,0,2:T(1,128)S(1)} fusion(f32[16,512,192]{1,0,2:T(8,128)} %get-tuple-element.682, s32[]{:T(128)S(6)} %select_n.149), kind=kLoop, calls=%fused_computation.16.clone.1 | loop fusion | bytes 786436 | tf_op jit(solution)/shard_map/while/body/eval_jaxpr/jit(dynamic_index_in_dim)/dynamic_slice | solution.py:19
  209.4 2.3 %constant_dynamic-slice_fusion.7 = f32[1,512,192]{1,0,2:T(1,128)S(1)} fusion(f32[16,512,192]{1,0,2:T(8,128)} %get-tuple-element.682, s32[]{:T(128)S(6)} %select_n.149), kind=kLoop, calls=%fused_computation.16.clone.1 | loop fusion | bytes 786436 | tf_op jit(solution)/shard_map/while/body/eval_jaxpr/jit(dynamic_index_in_dim)/dynamic_slice | solution.py:19
  211.9 2.3 %constant_dynamic-slice_fusion.7 = f32[1,512,192]{1,0,2:T(1,128)S(1)} fusion(f32[16,512,192]{1,0,2:T(8,128)} %get-tuple-element.682, s32[]{:T(128)S(6)} %select_n.149), kind=kLoop, calls=%fused_computation.16.clone.1 | loop fusion | bytes 786436 | tf_op jit(solution)/shard_map/while/body/eval_jaxpr/jit(dynamic_index_in_dim)/dynamic_slice | solution.py:19
  215.2 0.7 multiply_convert_fusion
  (102 shorter events, 6.5 us)
Async XLA Ops:
  7.2 27.8 %copy-start = (bf16[4096,192]{0,1:T(8,128)(2,1)S(1)}, bf16[4096,192]{0,1:T(8,128)(2,1)}, u32[]{:S(2)}) copy-start(bf16[4096,192]{0,1:T(8,128)(2,1)} %param.21) | copy-start | bytes 4718596
  9.7 0.6 copy-start.8
  37.6 2.5 %copy-start.10 = (s32[8,3]{0,1:T(4,128)S(1)}, s32[8,3]{0,1:T(4,128)}, u32[]{:S(2)}) copy-start(s32[8,3]{0,1:T(4,128)} %param.26) | copy-start | bytes 292
  52.8 16.9 %copy-start.9 = (s32[16,8]{1,0:T(8,128)S(1)}, s32[16,8]{1,0:T(8,128)}, u32[]{:S(2)}) copy-start(s32[16,8]{1,0:T(8,128)} %copy-done.8) | copy-start | bytes 1540
  52.8 16.9 %copy-start.12 = (s32[16]{0:T(128)S(1)}, s32[16]{0:T(128)}, u32[]{:S(2)}) copy-start(s32[16]{0:T(128)} %param.27) | copy-start | bytes 196
  56.3 9.8 %all-to-all-start.1 = ((bf16[16,1,128]{2,1,0:T(2,128)(2,1)}), bf16[16,1,128]{2,1,0:T(2,128)(2,1)S(1)}, u32[]{:S(2)}, u32[]{:S(2)}) async-start(bf16[16,1,128]{2,1,0:T(2,128)(2,1)} %copy.82), calls=%async_computation.1 | async-start | bytes 16384 | tf_op jit(solution)/shard_map/all_to_all | solution.py:127
  60.9 27.9 %copy-start.13 = (bf16[192,192]{1,0:T(8,128)(2,1)S(1)}, bf16[192,192]{1,0:T(8,128)(2,1)}, u32[]{:S(2)}) copy-start(bf16[192,192]{1,0:T(8,128)(2,1)} %param.31) | copy-start | bytes 221188
  66.1 22.3 %all-to-all-start = ((bf16[16,128,192]{1,2,0:T(8,128)(2,1)}), bf16[16,128,192]{1,2,0:T(8,128)(2,1)S(1)}, u32[]{:S(2)}, u32[]{:S(2)}) async-start(bf16[16,128,192]{1,2,0:T(8,128)(2,1)} %scatter_fusion), calls=%async_computation | async-start | bytes 1572864 | tf_op jit(solution)/shard_map/all_to_all | solution.py:126
  69.7 19.7 %copy-start.5 = (bf16[192,192]{1,0:T(8,128)(2,1)S(1)}, bf16[192,192]{1,0:T(8,128)(2,1)}, u32[]{:S(2)}) copy-start(bf16[192,192]{1,0:T(8,128)(2,1)} %param.32) | copy-start | bytes 221188
  69.7 95.1 %all-gather.5.cloned.1.call-start = ((), (), s32[]{:S(2)}) async-start(), calls=%async_computation.2 | async-start | bytes 6684672 | tf_op jit(solution)/shard_map/all_gather | solution.py:16
  70.1 19.6 %copy-start.6 = (bf16[192,192]{1,0:T(8,128)(2,1)S(1)}, bf16[192,192]{1,0:T(8,128)(2,1)}, u32[]{:S(2)}) copy-start(bf16[192,192]{1,0:T(8,128)(2,1)} %param.33) | copy-start | bytes 221188
  88.9 1.3 copy-start.3
  89.3 0.8 copy-start.4
  90.8 1.6 copy-start.1
  96.4 1.6 copy-start.1
  101.2 0.7 copy-start.2
  176.7 38.3 %copy-start.7 = (bf16[192,192]{1,0:T(8,128)(2,1)S(1)}, bf16[192,192]{1,0:T(8,128)(2,1)}, u32[]{:S(2)}) copy-start(bf16[192,192]{1,0:T(8,128)(2,1)} %param.34) | copy-start | bytes 221188
  176.7 38.5 %copy-start.11 = (f32[192]{0:T(256)S(1)}, f32[192]{0:T(256)}, u32[]{:S(2)}) copy-start(f32[192]{0:T(256)} %param.35) | copy-start | bytes 2308
Sparse Core Ops, SparseCore 0:
  102.1 62.6 all-gather.4
where the time goes:
time: 224 us; the launch traced here: 223 us
  local copies, waits for them, and re-layouts  70.7 us (32%)
  blocking collectives  64.8 us (29%)
  waiting for transfers between devices  42.9 us (19%)
  between operations  14.4 us (6%)
  matrix products  12 us (5%)
  other arithmetic  10.3 us (5%)
  starting transfers between devices  7.12 us (3%)
    all_gather x2, blocking collectives, merged_2(): gathered = jax.tree.map(lambda a: lax.all_gather(a, axis), part)  40.7 us
    dynamic_slice x18, local copies, waits for them, and re-layouts, take(): lax.dynamic_index_in_dim(a, source, 0, False)  35.2 us
    all_gather x1, blocking collectives, per_device(): everywhere = lax.all_gather(sn_positions, ('pts', 'sn'), axis=1, tiled=True)  24.1 us
    all_gather x1, waiting for transfers between devices, merged_2(): gathered = jax.tree.map(lambda a: lax.all_gather(a, axis), part)  22.1 us
    all_to_all x1, waiting for transfers between devices, per_device(): lax.all_to_all(outgoing, ('pts', 'sn'), split_axis=0, concat_axis=0, tile...  18.3 us
    unnamed x28, local copies, waits for them, and re-layouts  11.7 us
    dot_general x2, matrix products, block_attend(): jnp.einsum('lhk,khd->lhd', weights.astype(jnp.bfloat16), value_heads, pre...  5.27 us
  transfers between devices with their start and end apart: 3, of which 3 were waited for; matrix products, arithmetic and copies ran while one was open for 2% of the time, Pallas kernels for 0%

commit v1 on v0

v1 whole, which is shorter than its diff:
```python
import functools

import jax
import jax.numpy as jnp
from jax import lax
from jax.experimental import pallas as pl
from jax.experimental.pallas import tpu as pltpu
from jax.sharding import PartitionSpec as P

HEADS = 3
BLOCK = 128
INV_RADIUS_SQ = 100.0
MESH = pl.DeviceIdType.MESH
STAT_ROWS = 16
CHUNK = 512
LATENT_CHUNK = 256
OUT_LANES = 256
F32 = jnp.float32
BF16 = jnp.bfloat16


def contract(a, b, dim_a, dim_b):
    return lax.dot_general(a, b, (((dim_a,), (dim_b,)), ((), ())), preferred_element_type=F32)


def place(n_sn):
    return lax.axis_index("pts") * n_sn + lax.axis_index("sn")


def peer(index, n_sn):
    return {"pts": lax.div(index, n_sn), "sn": lax.rem(index, n_sn)}


def greet(owners, me, n_sn):
    barrier = pltpu.get_barrier_semaphore()

    def signal(off, carry):
        other = lax.rem(me + off, owners)
        pl.semaphore_signal(barrier, inc=1, device_id=peer(other, n_sn), device_id_type=MESH)
        return carry

    lax.fori_loop(1, owners, signal, 0)
    pl.semaphore_wait(barrier, owners - 1)


def columns_of(rows):
    padded = jnp.concatenate([rows, jnp.zeros((5, rows.shape[1]), F32)], axis=0)
    return jnp.transpose(padded)


def message_kernel(
    owners,
    n_sn,
    sn_blocks,
    targets,
    target_block,
    target_links,
    target_count,
    block_slot,
    feats,
    positions,
    sn_positions,
    w_in,
    w_mid,
    arrived,
    everywhere,
    hidden,
    point_blocks,
    outgoing,
    slots,
    pos_send,
    pos_recv,
    msg_send,
    msg_recv,
    own_sem,
):
    me = place(n_sn)
    links = target_links.shape[1]
    width = feats.shape[1]
    greet(owners, me, n_sn)

    def pos_copy(other, slot_at):
        return pltpu.make_async_remote_copy(
            src_ref=sn_positions,
            dst_ref=everywhere.at[slot_at],
            send_sem=pos_send.at[other],
            recv_sem=pos_recv.at[slot_at],
            device_id=peer(other, n_sn),
            device_id_type=MESH,
        )

    def start_pos(off, carry):
        pos_copy(lax.rem(me + off, owners), me).start()
        return carry

    lax.fori_loop(1, owners, start_pos, 0)
    own_pos = pltpu.make_async_copy(sn_positions, everywhere.at[me], own_sem.at[0])
    own_pos.start()

    def slot_of(k, carry):
        slots[k] = block_slot[target_block[me * targets + k]]
        return carry

    lax.fori_loop(0, targets, slot_of, 0)
    my_count = target_count[me]

    def mlp(step, carry):
        rows = feats[pl.ds(pl.multiple_of(step * CHUNK, CHUNK), CHUNK), :]
        inner = jax.nn.gelu(contract(w_in[...], rows, 0, 1)).astype(BF16)
        hid = contract(w_mid[...], inner, 0, 0).astype(BF16)
        places = positions[:, pl.ds(pl.multiple_of(step * CHUNK, CHUNK), CHUNK)]
        for q in range(CHUNK // BLOCK):
            hidden[step * (CHUNK // BLOCK) + q] = hid[:, q * BLOCK : (q + 1) * BLOCK]
            point_blocks[step * (CHUNK // BLOCK) + q] = places[:, q * BLOCK : (q + 1) * BLOCK]
        return carry

    lax.fori_loop(0, feats.shape[0] // CHUNK, mlp, 0)

    def wait_pos(off, carry):
        other = lax.rem(me + off, owners)
        copy = pos_copy(other, other)
        copy.wait_send()
        copy.wait_recv()
        return carry

    own_pos.wait()
    lax.fori_loop(1, owners, wait_pos, 0)

    def msg_copy(other, slot_at):
        return pltpu.make_async_remote_copy(
            src_ref=outgoing.at[other],
            dst_ref=arrived.at[slot_at],
            send_sem=msg_send.at[other],
            recv_sem=msg_recv.at[slot_at],
            device_id=peer(other, n_sn),
            device_id_type=MESH,
        )

    def build(other):
        def look(k, state):
            which, block, live = state
            slot = slots[k]
            hit = jnp.logical_and(lax.div(slot, sn_blocks) == other, k < my_count)
            return (
                jnp.where(hit, k, which),
                jnp.where(hit, lax.rem(slot, sn_blocks), block),
                jnp.where(hit, 1.0, live),
            )

        start = (jnp.int32(0), jnp.int32(0), F32(0.0))
        which, block, live = lax.fori_loop(0, targets, look, start, unroll=targets <= 8)
        candidates = everywhere[other]
        sn_rows = candidates[:, :BLOCK]
        for b in range(1, sn_blocks):
            sn_rows = jnp.where(block == b, candidates[:, b * BLOCK : (b + 1) * BLOCK], sn_rows)
        sn_cols = columns_of(sn_rows)
        kernels = []
        blocks = []
        for j in range(links):
            link = target_links[which, j]
            pts = point_blocks[link]
            dist = jnp.zeros((BLOCK, BLOCK), F32)
            for c in range(3):
                gap = sn_cols[:, c : c + 1] - pts[c : c + 1, :]
                dist = dist + gap * gap
            kernels.append(1.0 / (1.0 + dist * INV_RADIUS_SQ))
            blocks.append(hidden[link])
        total = kernels[0]
        for extra in kernels[1:]:
            total = total + extra
        total = jnp.sum(jnp.transpose(total), axis=0, keepdims=True)
        message = contract(
            jnp.concatenate(blocks, axis=1),
            jnp.concatenate([one.astype(BF16) for one in kernels], axis=1),
            1,
            1,
        )
        outgoing[other, :width, :] = (message * live).astype(BF16)
        outgoing[other, width:, :] = jnp.broadcast_to(total * live, (STAT_ROWS, BLOCK)).astype(BF16)

    def send(off, carry):
        other = lax.rem(me + off, owners)
        build(other)
        msg_copy(other, me).start()
        return carry

    lax.fori_loop(1, owners, send, 0)
    build(me)
    own = pltpu.make_async_copy(outgoing.at[me], arrived.at[me], own_sem.at[1])
    own.start()
    own.wait()

    def finish(off, carry):
        other = lax.rem(me + off, owners)
        copy = msg_copy(other, other)
        copy.wait_send()
        copy.wait_recv()
        return carry

    lax.fori_loop(1, owners, finish, 0)


def thirds(x):
    first = x.astype(BF16).astype(F32)
    second = (x - first).astype(BF16).astype(F32)
    third = x - first - second
    return [first, second, third]


def attend_kernel(
    owners,
    n_sn,
    sn_blocks,
    targets,
    target_block,
    block_slot,
    arrived,
    queries,
    w_post,
    w_key,
    w_value,
    features_out,
    partial_out,
    sums,
    pooled,
):
    me = place(n_sn)
    width = queries.shape[1]
    head_width = width // HEADS
    rows = queries.shape[0]
    sums[...] = jnp.zeros_like(sums)

    def add(source, carry):
        def look(k, block):
            slot = block_slot[target_block[source * targets + k]]
            return jnp.where(lax.div(slot, sn_blocks) == me, lax.rem(slot, sn_blocks), block)

        block = lax.fori_loop(0, targets, look, jnp.int32(0), unroll=targets <= 8)
        sums[block] += arrived[source].astype(F32)
        return carry

    lax.fori_loop(0, owners, add, 0)
    for b in range(sn_blocks):
        scale = 1.0 / (1.0 + sums[b, width : width + 1, :])
        pooled[:, b * BLOCK : (b + 1) * BLOCK] = (sums[b, :width, :] * scale).astype(BF16)
    features = jax.nn.gelu(contract(pooled[...], w_post[...], 0, 0)).astype(BF16)
    features_out[...] = features
    keys = contract(features, w_key[...], 1, 0).astype(BF16)
    values_t = contract(w_value[...], features, 0, 1).astype(BF16)
    head_of = lax.broadcasted_iota(jnp.int32, (LATENT_CHUNK, width), 1) // head_width
    for at in range(0, rows, LATENT_CHUNK):
        part = queries[at : at + LATENT_CHUNK, :] * BF16(head_width ** (-0.5))
        outs, peaks, totals = [], [], []
        for h in range(HEADS):
            scores = contract(keys, jnp.where(head_of == h, part, BF16(0.0)), 1, 1)
            peak = jnp.max(scores, axis=0, keepdims=True)
            probs = jnp.exp(scores - peak)
            totals += thirds(jnp.sum(probs, axis=0, keepdims=True))
            peaks += thirds(peak)
            outs.append(
                contract(
                    values_t[h * head_width : (h + 1) * head_width, :], probs.astype(BF16), 1, 0
                )
            )
        pad = jnp.zeros((OUT_LANES - width - 6 * HEADS, LATENT_CHUNK), F32)
        whole = jnp.concatenate(outs + peaks + totals + [pad], axis=0)
        partial_out[at : at + LATENT_CHUNK, :] = jnp.transpose(whole).astype(BF16)


def merge_kernel(
    owners, n_sn, parts, w_out, out_gain, latent_out, arrived, send_sem, recv_sem, own_sem
):
    me = place(n_sn)
    width = w_out.shape[0]
    head_width = width // HEADS
    share = parts.shape[1]
    greet(owners, me, n_sn)

    def copy_of(other, slot_at):
        return pltpu.make_async_remote_copy(
            src_ref=parts.at[other],
            dst_ref=arrived.at[slot_at],
            send_sem=send_sem.at[other],
            recv_sem=recv_sem.at[slot_at],
            device_id=peer(other, n_sn),
            device_id_type=MESH,
        )

    def start(off, carry):
        copy_of(lax.rem(me + off, owners), me).start()
        return carry

    lax.fori_loop(1, owners, start, 0)
    own = pltpu.make_async_copy(parts.at[me], arrived.at[me], own_sem)
    own.start()
    own.wait()

    def finish(off, carry):
        other = lax.rem(me + off, owners)
        copy = copy_of(other, other)
        copy.wait_send()
        copy.wait_recv()
        return carry

    lax.fori_loop(1, owners, finish, 0)
    head_of = lax.broadcasted_iota(jnp.int32, (share, width), 1) // head_width

    def spread(columns):
        full = jnp.broadcast_to(columns[HEADS - 1], (share, width))
        for h in range(HEADS - 2, -1, -1):
            full = jnp.where(head_of == h, columns[h], full)
        return full

    def stat(block, at):
        return spread(
            [
                block[:, at + 3 * h : at + 3 * h + 1]
                + block[:, at + 3 * h + 1 : at + 3 * h + 2]
                + block[:, at + 3 * h + 2 : at + 3 * h + 3]
                for h in range(HEADS)
            ]
        )

    def load(source):
        block = arrived[source].astype(F32)
        return block[:, :width], stat(block, width), stat(block, width + 3 * HEADS)

    def combine(source, state):
        output, peak, total = state
        new_output, new_peak, new_total = load(source)
        top = jnp.maximum(peak, new_peak)
        scale, new_scale = jnp.exp(peak - top), jnp.exp(new_peak - top)
        return (
            output * scale + new_output * new_scale,
            top,
            total * scale + new_total * new_scale,
        )

    output, peak, total = lax.fori_loop(1, owners, combine, load(0), unroll=owners <= 16)
    attended = (output / total).astype(BF16)
    projected = jnp.dot(attended, w_out[...], preferred_element_type=F32)
    mean_sq = jnp.mean(projected * projected, axis=-1, keepdims=True)
    latent_out[...] = (projected * lax.rsqrt(mean_sq + 1e-06) * out_gain[...]).astype(BF16)


def per_device(
    n_sn,
    owners,
    point_features,
    point_positions,
    sn_positions,
    latent_queries,
    target_block,
    target_links,
    target_count,
    block_slot,
    w_in,
    w_mid,
    w_post,
    w_key,
    w_value,
    w_out,
    out_gain,
):
    targets = target_links.shape[0]
    width = point_features.shape[1]
    sn_rows = sn_positions.shape[1]
    sn_blocks = sn_rows // BLOCK
    latents = latent_queries.shape[0]
    share = latents // owners
    smem = pl.BlockSpec(memory_space=pltpu.SMEM)
    vmem = pl.BlockSpec(memory_space=pltpu.VMEM)
    dma = pltpu.SemaphoreType.DMA
    arrived = pl.pallas_call(
        functools.partial(message_kernel, owners, n_sn, sn_blocks, targets),
        out_shape=jax.ShapeDtypeStruct((owners, width + STAT_ROWS, BLOCK), BF16),
        in_specs=[smem] * 4 + [vmem] * 5,
        out_specs=pl.BlockSpec(memory_space=pl.ANY),
        scratch_shapes=[
            pltpu.VMEM((owners, 3, sn_rows), F32),
            pltpu.VMEM((point_features.shape[0] // BLOCK, width, BLOCK), BF16),
            pltpu.VMEM((point_features.shape[0] // BLOCK, 3, BLOCK), F32),
            pltpu.VMEM((owners, width + STAT_ROWS, BLOCK), BF16),
            pltpu.SMEM((targets,), jnp.int32),
            dma((owners,)),
            dma((owners,)),
            dma((owners,)),
            dma((owners,)),
            dma((2,)),
        ],
        compiler_params=pltpu.CompilerParams(collective_id=0, has_side_effects=True),
        name="messages",
    )(
        target_block,
        target_links,
        target_count,
        block_slot,
        point_features,
        point_positions,
        sn_positions,
        w_in,
        w_mid,
    )
    features, partial = pl.pallas_call(
        functools.partial(attend_kernel, owners, n_sn, sn_blocks, targets),
        out_shape=(
            jax.ShapeDtypeStruct((sn_rows, width), BF16),
            jax.ShapeDtypeStruct((latents, OUT_LANES), BF16),
        ),
        in_specs=[smem] * 2 + [vmem] * 5,
        out_specs=(vmem, vmem),
        scratch_shapes=[
            pltpu.VMEM((sn_blocks, width + STAT_ROWS, BLOCK), F32),
            pltpu.VMEM((width, sn_rows), BF16),
        ],
        name="attend",
    )(target_block, block_slot, arrived, latent_queries, w_post, w_key, w_value)
    latent_out = pl.pallas_call(
        functools.partial(merge_kernel, owners, n_sn),
        out_shape=jax.ShapeDtypeStruct((share, width), BF16),
        in_specs=[vmem] * 3,
        out_specs=vmem,
        scratch_shapes=[
            pltpu.VMEM((owners, share, OUT_LANES), BF16),
            dma((owners,)),
            dma((owners,)),
            dma,
        ],
        compiler_params=pltpu.CompilerParams(collective_id=1, has_side_effects=True),
        name="merge",
    )(partial.reshape(owners, share, OUT_LANES), w_out, out_gain.reshape(1, width))
    return (features, latent_out)


def solution(mesh):
    n_sn = mesh.shape["sn"]
    owners = mesh.shape["pts"] * n_sn
    everything = ("groups", "pts", "sn")
    in_specs = (
        P(everything, None),
        P(None, everything),
        P(None, everything),
        P(),
        P("groups"),
        P(everything, None),
        P("groups"),
        P("groups"),
        P(),
        P(),
        P(),
        P(),
        P(),
        P(),
        P(),
    )
    out_specs = (P(everything, None), P(everything, None))
    return jax.shard_map(
        functools.partial(per_device, n_sn, owners),
        mesh=mesh,
        in_specs=in_specs,
        out_specs=out_specs,
        check_vma=False,
    )
```

time: 224 us -> 64.9 us (0.29)
  blocking collectives: 64.8 us -> 0 us
  local copies, waits for them, and re-layouts: 70.7 us -> 8.68 us
  Pallas kernels: 0 us -> 54.6 us
  waiting for transfers between devices: 42.9 us -> 0 us
  between operations: 14.4 us -> 0.66 us
  matrix products: 12 us -> 0 us
  other arithmetic: 10.3 us -> 0 us
  starting transfers between devices: 7.12 us -> 0 us
    all_gather x3 -> x0, blocking collectives: 64.8 us -> none  [the longest x2 40.7 us: merged_2(): gathered = jax.tree.map(lambda a: lax.all_gather(a, axis), part)]
    pallas_call x0 -> x3, Pallas kernels: none -> 54.6 us  [the longest x1 30.7 us: per_device(): pl.pallas_call(functools.partial(message_kernel, owners, n_sn, sn_blocks,...]
    dynamic_slice x23 -> x0, local copies, waits for them, and re-layouts: 36.8 us -> none  [the longest x18 35.2 us: take(): lax.dynamic_index_in_dim(a, source, 0, False)]
    all_gather x1 -> x0, waiting for transfers between devices: 22.1 us -> none  [merged_2(): gathered = jax.tree.map(lambda a: lax.all_gather(a, axis), part)]
    all_to_all x2 -> x0, waiting for transfers between devices: 20.8 us -> none  [the longest x1 18.3 us: per_device(): lax.all_to_all(outgoing, ('pts', 'sn'), split_axis=0, concat_axis=0, tile...]
    dot_general x13 -> x0, matrix products: 12 us -> none  [the longest x2 5.27 us: block_attend(): jnp.einsum('lhk,khd->lhd', weights.astype(jnp.bfloat16), value_heads, pre...]
    gather x8 -> x0, local copies, waits for them, and re-layouts: 9.38 us -> none  [the longest x2 4.38 us: one_batch(): feats = hidden_blocks[link_ids]]
    all_to_all x2 -> x0, starting transfers between devices: 7.08 us -> none  [the longest x1 3.61 us: per_device(): lax.all_to_all(outgoing, ('pts', 'sn'), split_axis=0, concat_axis=0, tile...]
  transfers between devices with their start and end apart: 3 -> 0, of which waited for: 3 -> 0; matrix products, arithmetic and copies ran while one was open for 2% -> 0% of each run, Pallas kernels for 0% -> 0%
where the time goes in v1:
time: 64.9 us; the launch traced here: 64 us
  Pallas kernels  54.6 us (84%)
  local copies, waits for them, and re-layouts  8.68 us (13%)
  between operations  0.66 us (1%)
    pallas_call x1, Pallas kernels, per_device(): pl.pallas_call(functools.partial(message_kernel, owners, n_sn, sn_blocks,...  30.7 us
    pallas_call x1, Pallas kernels, per_device(): pl.pallas_call(functools.partial(merge_kernel, owners, n_sn), out_shape=j...  16.8 us
    unnamed x9, local copies, waits for them, and re-layouts  8.68 us
    pallas_call x1, Pallas kernels, per_device(): pl.pallas_call(functools.partial(attend_kernel, owners, n_sn, sn_blocks,...  7.1 us

profile of v1, /device:TPU:0, one launch (start us, length us, event | category | flops | bytes accessed | tf_op | source)
XLA Modules:
  0.0 64.0 jit_solution(15695363613219734103)
XLA Ops:
  0.6 0.0 copy-start.1
  0.6 3.9 %copy.18.feats = bf16[4096,192]{1,0:T(8,128)(2,1)} copy(bf16[4096,192]{0,1:T(8,128)(2,1)} %param.15) | data formatting | bytes 3145728 | tf_op args[0]
  4.5 0.0 copy-done.1
  4.5 0.0 copy-start
  4.5 0.7 %copy.17.target_links = s32[8,3]{1,0:T(8,128)} copy(s32[8,3]{0,1:T(4,128)S(1)} %copy-done.1) | data formatting | bytes 192 | tf_op args[5]
  5.2 30.7 %messages.1.arrived = bf16[16,208,128]{2,1,0:T(8,128)(2,1)} custom-call(s32[128]{0:T(128)} %target_block.3, s32[8,3]{1,0:T(8,128)} %copy.17.target_links, s32[16]{0:T(128)} %target_count.1, s32[128]{0:T(128)} %block_slot.3, bf16[4096,192]{1,0:T(8,128)(2,1)} %copy.18.feats, f32[3,4096]{1,0:T(4,128)} %positions.1, f32[3,1024]{1,0:T(4,128)} %sn_positions.1, ...), custom_call_target="tpu_custom_call" | custom-call | tf_op jit(solution)/shard_map/messages/pallas_call | solution.py:374
  35.9 0.0 copy-done
  35.9 0.8 %copy.19.queries = bf16[512,192]{1,0:T(8,128)(2,1)} copy(bf16[512,192]{0,1:T(8,128)(2,1)S(1)} %copy-done) | data formatting | bytes 393216 | tf_op args[3]
  36.7 7.1 %attend.1 = (bf16[1024,192]{1,0:T(8,128)(2,1)}, bf16[512,256]{1,0:T(8,128)(2,1)}) custom-call(s32[128]{0:T(128)} %target_block.3, s32[128]{0:T(128)} %block_slot.3, bf16[16,208,128]{2,1,0:T(8,128)(2,1)} %messages.1.arrived, bf16[512,192]{1,0:T(8,128)(2,1)} %copy.19.queries, bf16[192,192]{1,0:T(8,128)(2,1)} %w_post.1, bf16[192,192]{1,0:T(8,128)(2,1)} %w_key.1, ...), custom_call_target="tpu_custom_call" | custom-call | tf_op jit(solution)/shard_map/attend/pallas_call | solution.py:404
  43.8 2.0 %copy.20 = bf16[1024,192]{0,1:T(8,128)(2,1)} copy(bf16[1024,192]{1,0:T(8,128)(2,1)} %get-tuple-element.6) | data formatting | bytes 786432
  45.8 16.8 %merge.1 = bf16[32,192]{1,0:T(8,128)(2,1)} custom-call(bf16[16,32,256]{2,1,0:T(8,128)(2,1)} %bitcast.2, bf16[192,192]{1,0:T(8,128)(2,1)} %w_out.1, f32[1,192]{1,0:T(1,128)} %bitcast.3), custom_call_target="tpu_custom_call" | custom-call | tf_op jit(solution)/shard_map/merge/pallas_call | solution.py:418
  62.6 1.3 %copy.22 = bf16[32,192]{1,0:T(8,128)(2,1)} copy(bf16[32,192]{1,0:T(8,128)(2,1)} %merge.1) | data formatting | bytes 24576
Async XLA Ops:
  0.6 3.9 %copy-start.1 = (s32[8,3]{0,1:T(4,128)S(1)}, s32[8,3]{0,1:T(4,128)}, u32[]{:S(2)}) copy-start(s32[8,3]{0,1:T(4,128)} %param.20) | copy-start | bytes 292
  4.5 31.4 %copy-start = (bf16[512,192]{0,1:T(8,128)(2,1)S(1)}, bf16[512,192]{0,1:T(8,128)(2,1)}, u32[]{:S(2)}) copy-start(bf16[512,192]{0,1:T(8,128)(2,1)} %param.18) | copy-start | bytes 589828

commit v2 on v1

v2 whole, which is shorter than its diff:
```python
import functools

import jax
import jax.numpy as jnp
from jax import lax
from jax.experimental import pallas as pl
from jax.experimental.pallas import tpu as pltpu
from jax.sharding import PartitionSpec as P

HEADS = 3
BLOCK = 128
INV_RADIUS_SQ = 100.0
MESH = pl.DeviceIdType.MESH
STAT_ROWS = 8
CHUNK = 512
LATENT_CHUNK = 256
OUT_LANES = 256
F32 = jnp.float32
BF16 = jnp.bfloat16


def contract(a, b, dim_a, dim_b):
    return lax.dot_general(a, b, (((dim_a,), (dim_b,)), ((), ())), preferred_element_type=F32)


def place(n_sn):
    return lax.axis_index("pts") * n_sn + lax.axis_index("sn")


def peer(index, n_sn):
    return {"pts": lax.div(index, n_sn), "sn": lax.rem(index, n_sn)}


def greet(owners, me, n_sn):
    barrier = pltpu.get_barrier_semaphore()

    def signal(off, carry):
        other = lax.rem(me + off, owners)
        pl.semaphore_signal(barrier, inc=1, device_id=peer(other, n_sn), device_id_type=MESH)
        return carry

    lax.fori_loop(1, owners, signal, 0)
    return barrier


def far_first(i, owners):
    return owners // 2 + lax.div(i + 1, 2) * (2 * lax.rem(i + 1, 2) - 1)


def named_block(owner, targets, sn_blocks, count, slot_at):
    def look(k, state):
        which, block, live = state
        slot = slot_at(k)
        hit = jnp.logical_and(lax.div(slot, sn_blocks) == owner, k < count)
        return (
            jnp.where(hit, k, which),
            jnp.where(hit, lax.rem(slot, sn_blocks), block),
            jnp.where(hit, 1.0, live),
        )

    start = (jnp.int32(0), jnp.int32(0), F32(0.0))
    return lax.fori_loop(0, targets, look, start, unroll=targets <= 8)


def columns_of(rows):
    padded = jnp.concatenate([rows, jnp.zeros((5, rows.shape[1]), F32)], axis=0)
    return jnp.transpose(padded)


def message_kernel(
    owners,
    n_sn,
    sn_blocks,
    targets,
    target_block,
    target_links,
    target_count,
    block_slot,
    feats,
    positions,
    sn_positions,
    w_in,
    w_mid,
    arrived,
    points,
    wanted,
    everywhere,
    hidden,
    point_blocks,
    outgoing,
    slots,
    pos_send,
    pos_recv,
    msg_send,
    msg_recv,
    own_sem,
):
    me = place(n_sn)
    links = target_links.shape[0]
    width = feats.shape[0]
    barrier = greet(owners, me, n_sn)
    load = pltpu.make_async_copy(feats, points, own_sem.at[2])
    load.start()

    def choose(region, carry):
        def slot_at(k):
            return block_slot[target_block[region * targets + k]]

        block = named_block(me, targets, sn_blocks, target_count[region], slot_at)[1]
        rows = sn_positions[:, :BLOCK]
        for b in range(1, sn_blocks):
            rows = jnp.where(block == b, sn_positions[:, b * BLOCK : (b + 1) * BLOCK], rows)
        wanted[region] = rows
        return carry

    lax.fori_loop(0, owners, choose, 0)

    def slot_of(k, carry):
        slots[k] = block_slot[target_block[me * targets + k]]
        return carry

    lax.fori_loop(0, targets, slot_of, 0)
    my_count = target_count[me]

    def pos_copy(other, slot_at):
        return pltpu.make_async_remote_copy(
            src_ref=wanted.at[other],
            dst_ref=everywhere.at[slot_at],
            send_sem=pos_send.at[other],
            recv_sem=pos_recv.at[slot_at],
            device_id=peer(other, n_sn),
            device_id_type=MESH,
        )

    def start_pos(i, carry):
        pos_copy(lax.rem(me + far_first(i, owners), owners), me).start()
        return carry

    pl.semaphore_wait(barrier, owners - 1)
    lax.fori_loop(0, owners - 1, start_pos, 0)
    own_pos = pltpu.make_async_copy(wanted.at[me], everywhere.at[me], own_sem.at[0])
    own_pos.start()
    load.wait()

    def mlp(step, carry):
        span = pl.ds(pl.multiple_of(step * CHUNK, CHUNK), CHUNK)
        inner = jax.nn.gelu(contract(w_in[...], points[:, span], 0, 0)).astype(BF16)
        hid = contract(w_mid[...], inner, 0, 0).astype(BF16)
        places = positions[:, span]
        for q in range(CHUNK // BLOCK):
            hidden[step * (CHUNK // BLOCK) + q] = hid[:, q * BLOCK : (q + 1) * BLOCK]
            point_blocks[step * (CHUNK // BLOCK) + q] = places[:, q * BLOCK : (q + 1) * BLOCK]
        return carry

    lax.fori_loop(0, feats.shape[1] // CHUNK, mlp, 0)

    def wait_pos(off, carry):
        other = lax.rem(me + off, owners)
        copy = pos_copy(other, other)
        copy.wait_send()
        copy.wait_recv()
        return carry

    own_pos.wait()
    lax.fori_loop(1, owners, wait_pos, 0)

    def msg_copy(other, slot_at):
        return pltpu.make_async_remote_copy(
            src_ref=outgoing.at[other],
            dst_ref=arrived.at[slot_at],
            send_sem=msg_send.at[other],
            recv_sem=msg_recv.at[slot_at],
            device_id=peer(other, n_sn),
            device_id_type=MESH,
        )

    def build(other):
        which, block, live = named_block(
            other, targets, sn_blocks, my_count, lambda k: slots[k]
        )
        sn_cols = columns_of(everywhere[other])
        kernels = []
        blocks = []
        for j in range(links):
            link = target_links[j, which]
            pts = point_blocks[link]
            dist = jnp.zeros((BLOCK, BLOCK), F32)
            for c in range(3):
                gap = sn_cols[:, c : c + 1] - pts[c : c + 1, :]
                dist = dist + gap * gap
            kernels.append(1.0 / (1.0 + dist * INV_RADIUS_SQ))
            blocks.append(hidden[link])
        total = kernels[0]
        for extra in kernels[1:]:
            total = total + extra
        total = jnp.sum(jnp.transpose(total), axis=0, keepdims=True)
        message = contract(
            jnp.concatenate(blocks, axis=1),
            jnp.concatenate([one.astype(BF16) for one in kernels], axis=1),
            1,
            1,
        )
        outgoing[other, :width, :] = (message * live).astype(BF16)
        outgoing[other, width:, :] = jnp.broadcast_to(total * live, (STAT_ROWS, BLOCK)).astype(BF16)

    def nth(i):
        return lax.rem(me + far_first(i, owners), owners)

    build(nth(0))

    def send(i, carry):
        build(nth(i))
        msg_copy(nth(i - 1), me).start()
        return carry

    lax.fori_loop(1, owners - 1, send, 0)
    build(me)
    msg_copy(nth(owners - 2), me).start()
    own = pltpu.make_async_copy(outgoing.at[me], arrived.at[me], own_sem.at[1])
    own.start()
    own.wait()

    def finish(off, carry):
        other = lax.rem(me + off, owners)
        copy = msg_copy(other, other)
        copy.wait_send()
        copy.wait_recv()
        return carry

    lax.fori_loop(1, owners, finish, 0)


def thirds(x):
    first = x.astype(BF16).astype(F32)
    second = (x - first).astype(BF16).astype(F32)
    third = x - first - second
    return [first, second, third]


def pool_kernel(
    owners, n_sn, sn_blocks, targets, target_block, block_slot, arrived, w_post, features_out, sums, pooled
):
    me = place(n_sn)
    width = w_post.shape[0]
    sums[...] = jnp.zeros_like(sums)

    def add(source, carry):
        def look(k, block):
            slot = block_slot[target_block[source * targets + k]]
            return jnp.where(lax.div(slot, sn_blocks) == me, lax.rem(slot, sn_blocks), block)

        block = lax.fori_loop(0, targets, look, jnp.int32(0), unroll=targets <= 8)
        sums[block] += arrived[source].astype(F32)
        return carry

    lax.fori_loop(0, owners, add, 0)
    for b in range(sn_blocks):
        scale = 1.0 / (1.0 + sums[b, width : width + 1, :])
        pooled[:, b * BLOCK : (b + 1) * BLOCK] = (sums[b, :width, :] * scale).astype(BF16)
    features_out[...] = jax.nn.gelu(contract(w_post[...], pooled[...], 0, 0)).astype(BF16)


def attend_kernel(
    owners,
    n_sn,
    features,
    queries,
    w_key,
    w_value,
    w_out,
    out_gain,
    latent_out,
    values_t,
    keys,
    parts,
    arrived,
    send_sem,
    recv_sem,
    own_sem,
):
    me = place(n_sn)
    width, latents = queries.shape
    head_width = width // HEADS
    share = latents // owners
    chunks = latents // LATENT_CHUNK
    per_chunk = LATENT_CHUNK // share
    barrier = greet(owners, me, n_sn)
    keys[...] = contract(features[...], w_key[...], 0, 0).astype(BF16)
    values_t[...] = contract(w_value[...], features[...], 0, 0).astype(BF16)
    row_head = lax.broadcasted_iota(jnp.int32, (width, LATENT_CHUNK), 0) // head_width
    first = lax.div(me, per_chunk) + chunks // 2

    def attend(step, carry):
        chunk = lax.rem(first + step, chunks)
        at = pl.multiple_of(chunk * LATENT_CHUNK, LATENT_CHUNK)
        part = queries[:, pl.ds(at, LATENT_CHUNK)] * BF16(head_width ** (-0.5))
        outs, peaks, totals = [], [], []
        for h in range(HEADS):
            scores = contract(keys[...], jnp.where(row_head == h, part, BF16(0.0)), 1, 0)
            peak = jnp.max(scores, axis=0, keepdims=True)
            probs = jnp.exp(scores - peak)
            totals += thirds(jnp.sum(probs, axis=0, keepdims=True))
            peaks += thirds(peak)
            own_values = values_t[h * head_width : (h + 1) * head_width, :]
            outs.append(contract(own_values, probs.astype(BF16), 1, 0))
        pad = jnp.zeros((OUT_LANES - width - 6 * HEADS, LATENT_CHUNK), F32)
        whole = jnp.transpose(jnp.concatenate(outs + peaks + totals + [pad], axis=0))
        for j in range(per_chunk):
            parts[chunk * per_chunk + j] = whole[j * share : (j + 1) * share, :].astype(BF16)
        return carry

    def copy_of(other, slot_at):
        return pltpu.make_async_remote_copy(
            src_ref=parts.at[other],
            dst_ref=arrived.at[slot_at],
            send_sem=send_sem.at[other],
            recv_sem=recv_sem.at[slot_at],
            device_id=peer(other, n_sn),
            device_id_type=MESH,
        )

    def send_chunk(step):
        chunk = lax.rem(first + step, chunks)

        def start(j, carry):
            other = chunk * per_chunk + lax.rem(me + j, per_chunk)

            @pl.when(other != me)
            def _():
                copy_of(other, me).start()

            return carry

        lax.fori_loop(0, per_chunk, start, 0)

    attend(0, 0)
    pl.semaphore_wait(barrier, owners - 1)

    def step_on(step, carry):
        send_chunk(step - 1)
        return attend(step, carry)

    lax.fori_loop(1, chunks, step_on, 0)
    send_chunk(chunks - 1)
    own = pltpu.make_async_copy(parts.at[me], arrived.at[me], own_sem)
    own.start()
    own.wait()

    def finish(off, carry):
        other = lax.rem(me + off, owners)
        copy = copy_of(other, other)
        copy.wait_send()
        copy.wait_recv()
        return carry

    lax.fori_loop(1, owners, finish, 0)
    lane = lax.broadcasted_iota(jnp.int32, (OUT_LANES, width), 0) - width
    head_of = lax.broadcasted_iota(jnp.int32, (OUT_LANES, width), 1) // head_width
    is_peak = jnp.logical_and(lane >= 3 * head_of, lane < 3 * head_of + 3)
    total_lane = lane - 3 * HEADS
    is_total = jnp.logical_and(total_lane >= 3 * head_of, total_lane < 3 * head_of + 3)
    flat = jnp.concatenate([arrived[source] for source in range(owners)], axis=0)
    peaks = contract(flat, jnp.where(is_peak, 1.0, 0.0).astype(BF16), 1, 0)
    totals = contract(flat, jnp.where(is_total, 1.0, 0.0).astype(BF16), 1, 0)

    def of(full, source):
        return full[source * share : (source + 1) * share, :]

    top = of(peaks, 0)
    for source in range(1, owners):
        top = jnp.maximum(top, of(peaks, source))
    output = jnp.zeros((share, width), F32)
    total = jnp.zeros((share, width), F32)
    for source in range(owners):
        scale = jnp.exp(of(peaks, source) - top)
        output = output + scale * arrived[source][:, :width].astype(F32)
        total = total + scale * of(totals, source)
    attended = (output / total).astype(BF16)
    projected = jnp.dot(attended, w_out[...], preferred_element_type=F32)
    mean_sq = jnp.mean(projected * projected, axis=-1, keepdims=True)
    latent_out[...] = (projected * lax.rsqrt(mean_sq + 1e-06) * out_gain[...]).astype(BF16)


def per_device(
    n_sn,
    owners,
    point_features,
    point_positions,
    sn_positions,
    latent_queries,
    target_block,
    target_links,
    target_count,
    block_slot,
    w_in,
    w_mid,
    w_post,
    w_key,
    w_value,
    w_out,
    out_gain,
):
    targets = target_links.shape[0]
    width = point_features.shape[1]
    sn_rows = sn_positions.shape[1]
    sn_blocks = sn_rows // BLOCK
    latents = latent_queries.shape[0]
    share = latents // owners
    smem = pl.BlockSpec(memory_space=pltpu.SMEM)
    vmem = pl.BlockSpec(memory_space=pltpu.VMEM)
    hbm = pl.BlockSpec(memory_space=pl.ANY)
    dma = pltpu.SemaphoreType.DMA
    arrived = pl.pallas_call(
        functools.partial(message_kernel, owners, n_sn, sn_blocks, targets),
        out_shape=jax.ShapeDtypeStruct((owners, width + STAT_ROWS, BLOCK), BF16),
        in_specs=[smem] * 4 + [hbm] + [vmem] * 4,
        out_specs=pl.BlockSpec(memory_space=pl.ANY),
        scratch_shapes=[
            pltpu.VMEM(point_features.shape[::-1], BF16),
            pltpu.VMEM((owners, 3, BLOCK), F32),
            pltpu.VMEM((owners, 3, BLOCK), F32),
            pltpu.VMEM((point_features.shape[0] // BLOCK, width, BLOCK), BF16),
            pltpu.VMEM((point_features.shape[0] // BLOCK, 3, BLOCK), F32),
            pltpu.VMEM((owners, width + STAT_ROWS, BLOCK), BF16),
            pltpu.SMEM((targets,), jnp.int32),
            dma((owners,)),
            dma((owners,)),
            dma((owners,)),
            dma((owners,)),
            dma((3,)),
        ],
        compiler_params=pltpu.CompilerParams(collective_id=0, has_side_effects=True),
        name="messages",
    )(
        target_block,
        target_links.T,
        target_count,
        block_slot,
        point_features.T,
        point_positions,
        sn_positions,
        w_in,
        w_mid,
    )
    features_t = pl.pallas_call(
        functools.partial(pool_kernel, owners, n_sn, sn_blocks, targets),
        out_shape=jax.ShapeDtypeStruct((width, sn_rows), BF16),
        in_specs=[smem] * 2 + [vmem] * 2,
        out_specs=vmem,
        scratch_shapes=[
            pltpu.VMEM((sn_blocks, width + STAT_ROWS, BLOCK), F32),
            pltpu.VMEM((width, sn_rows), BF16),
        ],
        name="pool",
    )(target_block, block_slot, arrived, w_post)
    latent_out = pl.pallas_call(
        functools.partial(attend_kernel, owners, n_sn),
        out_shape=jax.ShapeDtypeStruct((share, width), BF16),
        in_specs=[vmem] * 6,
        out_specs=vmem,
        scratch_shapes=[
            pltpu.VMEM((width, sn_rows), BF16),
            pltpu.VMEM((sn_rows, width), BF16),
            pltpu.VMEM((owners, share, OUT_LANES), BF16),
            pltpu.VMEM((owners, share, OUT_LANES), BF16),
            dma((owners,)),
            dma((owners,)),
            dma,
        ],
        compiler_params=pltpu.CompilerParams(collective_id=1, has_side_effects=True),
        name="attend",
    )(features_t, latent_queries.T, w_key, w_value, w_out, out_gain.reshape(1, width))
    return (features_t.T, latent_out)


def solution(mesh):
    n_sn = mesh.shape["sn"]
    owners = mesh.shape["pts"] * n_sn
    everything = ("groups", "pts", "sn")
    in_specs = (
        P(everything, None),
        P(None, everything),
        P(None, everything),
        P(),
        P("groups"),
        P(everything, None),
        P("groups"),
        P("groups"),
        P(),
        P(),
        P(),
        P(),
        P(),
        P(),
        P(),
    )
    out_specs = (P(everything, None), P(everything, None))
    return jax.shard_map(
        functools.partial(per_device, n_sn, owners),
        mesh=mesh,
        in_specs=in_specs,
        out_specs=out_specs,
        check_vma=False,
    )
```

time: 64.9 us -> 50.1 us (0.77); the launches traced: 64 us -> 49.8 us
  local copies, waits for them, and re-layouts: 8.68 us -> 1.32 us
  Pallas kernels: 54.6 us -> 47.9 us
    unnamed x9 -> x1, local copies, waits for them, and re-layouts: 8.68 us -> 1.32 us
    pallas_call x2, Pallas kernels: 23.9 us -> 17.9 us  [the longest x1 14.8 us: per_device(): pl.pallas_call(functools.partial(attend_kernel, owners, n_sn), out_shape=...]
    pallas_call x1, Pallas kernels: 30.7 us -> 29.9 us  [per_device(): pl.pallas_call(functools.partial(message_kernel, owners, n_sn, sn_blocks,...]
where the time goes in v2:
time: 50.1 us; the launch traced here: 49.8 us
  Pallas kernels  47.9 us (96%)
  local copies, waits for them, and re-layouts  1.32 us (3%)
  between operations  0.65 us (1%)
    pallas_call x1, Pallas kernels, per_device(): pl.pallas_call(functools.partial(message_kernel, owners, n_sn, sn_blocks,...  29.9 us
    pallas_call x1, Pallas kernels, per_device(): pl.pallas_call(functools.partial(attend_kernel, owners, n_sn), out_shape=...  14.8 us
    pallas_call x1, Pallas kernels, per_device(): pl.pallas_call(functools.partial(pool_kernel, owners, n_sn, sn_blocks, ta...  3.12 us
    unnamed x1, local copies, waits for them, and re-layouts  1.32 us

profile of v2, /device:TPU:0, one launch (start us, length us, event | category | flops | bytes accessed | tf_op | source)
XLA Modules:
  0.0 49.8 jit_solution(6250917439678407707)
XLA Ops:
  0.6 29.9 %messages.1.arrived = bf16[16,200,128]{2,1,0:T(8,128)(2,1)} custom-call(s32[128]{0:T(128)} %target_block.3, s32[3,8]{1,0:T(4,128)} %bitcast.8, s32[16]{0:T(128)} %target_count.1, s32[128]{0:T(128)} %block_slot.3, bf16[192,4096]{1,0:T(8,128)(2,1)} %bitcast.5, f32[3,4096]{1,0:T(4,128)} %positions.1, f32[3,1024]{1,0:T(4,128)} %sn_positions.1, ...), custom_call_target="tpu_custom_call" | custom-call | tf_op jit(solution)/shard_map/messages/pallas_call | solution.py:413
  30.6 3.1 %pool.1.features = bf16[192,1024]{1,0:T(8,128)(2,1)} custom-call(s32[128]{0:T(128)} %target_block.3, s32[128]{0:T(128)} %block_slot.3, bf16[16,200,128]{2,1,0:T(8,128)(2,1)} %messages.1.arrived, bf16[192,192]{1,0:T(8,128)(2,1)} %w_post.1), custom_call_target="tpu_custom_call" | custom-call | tf_op jit(solution)/shard_map/pool/pallas_call | solution.py:445
  33.7 14.8 %attend.1 = bf16[32,192]{1,0:T(8,128)(2,1)} custom-call(bf16[192,1024]{1,0:T(8,128)(2,1)} %pool.1.features, bf16[192,512]{1,0:T(8,128)(2,1)} %bitcast.7, bf16[192,192]{1,0:T(8,128)(2,1)} %w_key.1, bf16[192,192]{1,0:T(8,128)(2,1)} %w_value.1, bf16[192,192]{1,0:T(8,128)(2,1)} %w_out.1, f32[1,192]{1,0:T(1,128)} %bitcast.9), custom_call_target="tpu_custom_call" | custom-call | tf_op jit(solution)/shard_map/attend/pallas_call | solution.py:456
  48.5 1.3 %copy.18 = bf16[32,192]{1,0:T(8,128)(2,1)} copy(bf16[32,192]{1,0:T(8,128)(2,1)} %attend.1) | data formatting | bytes 24576

commit v3 on v2

--- a/solution.py
+++ b/solution.py
@@ -81,7 +81,10 @@
     sn_positions,
     w_in,
     w_mid,
+    pooled,
     arrived,
+    sums,
+    block_of,
     points,
     wanted,
     everywhere,
@@ -107,6 +110,7 @@
             return block_slot[target_block[region * targets + k]]
 
         block = named_block(me, targets, sn_blocks, target_count[region], slot_at)[1]
+        block_of[region] = block
         rows = sn_positions[:, :BLOCK]
         for b in range(1, sn_blocks):
             rows = jnp.where(block == b, sn_positions[:, b * BLOCK : (b + 1) * BLOCK], rows)
@@ -153,16 +157,6 @@
         return carry
 
     lax.fori_loop(0, feats.shape[1] // CHUNK, mlp, 0)
-
-    def wait_pos(off, carry):
-        other = lax.rem(me + off, owners)
-        copy = pos_copy(other, other)
-        copy.wait_send()
-        copy.wait_recv()
-        return carry
-
-    own_pos.wait()
-    lax.fori_loop(1, owners, wait_pos, 0)
 
     def msg_copy(other, slot_at):
         return pltpu.make_async_remote_copy(
@@ -206,28 +200,51 @@
     def nth(i):
         return lax.rem(me + far_first(i, owners), owners)
 
-    build(nth(0))
+    def build_next(i):
+        pos_copy(nth(i), nth(i)).wait_recv()
+        build(nth(i))
+
+    build_next(0)
 
     def send(i, carry):
-        build(nth(i))
+        build_next(i)
         msg_copy(nth(i - 1), me).start()
         return carry
 
     lax.fori_loop(1, owners - 1, send, 0)
+    own_pos.wait()
     build(me)
     msg_copy(nth(owners - 2), me).start()
     own = pltpu.make_async_copy(outgoing.at[me], arrived.at[me], own_sem.at[1])
     own.start()
     own.wait()
 
-    def finish(off, carry):
-        other = lax.rem(me + off, owners)
-        copy = msg_copy(other, other)
-        copy.wait_send()
+    def add(source):
+        block = block_of[source]
+        message = arrived[source].astype(F32)
+        for b in range(sn_blocks):
+            sums[b] += jnp.where(block == b, message, 0.0)
+
+    sums[...] = jnp.zeros_like(sums)
+    add(me)
+
+    def finish(i, carry):
+        copy = msg_copy(nth(owners - 2 - i), nth(owners - 2 - i))
         copy.wait_recv()
-        return carry
-
-    lax.fori_loop(1, owners, finish, 0)
+        add(nth(owners - 2 - i))
+        return carry
+
+    lax.fori_loop(0, owners - 1, finish, 0)
+
+    def sent(i, carry):
+        msg_copy(nth(i), nth(i)).wait_send()
+        pos_copy(nth(i), nth(i)).wait_send()
+        return carry
+
+    lax.fori_loop(0, owners - 1, sent, 0)
+    for b in range(sn_blocks):
+        scale = 1.0 / (1.0 + sums[b, width : width + 1, :])
+        pooled[:, b * BLOCK : (b + 1) * BLOCK] = (sums[b, :width, :] * scale).astype(BF16)
 
 
 def thirds(x):
@@ -237,26 +254,7 @@
     return [first, second, third]
 
 
-def pool_kernel(
-    owners, n_sn, sn_blocks, targets, target_block, block_slot, arrived, w_post, features_out, sums, pooled
-):
-    me = place(n_sn)
-    width = w_post.shape[0]
-    sums[...] = jnp.zeros_like(sums)
-
-    def add(source, carry):
-        def look(k, block):
-            slot = block_slot[target_block[source * targets + k]]
-            return jnp.where(lax.div(slot, sn_blocks) == me, lax.rem(slot, sn_blocks), block)
-
-        block = lax.fori_loop(0, targets, look, jnp.int32(0), unroll=targets <= 8)
-        sums[block] += arrived[source].astype(F32)
-        return carry
-
-    lax.fori_loop(0, owners, add, 0)
-    for b in range(sn_blocks):
-        scale = 1.0 / (1.0 + sums[b, width : width + 1, :])
-        pooled[:, b * BLOCK : (b + 1) * BLOCK] = (sums[b, :width, :] * scale).astype(BF16)
+def post_kernel(pooled, w_post, features_out):
     features_out[...] = jax.nn.gelu(contract(w_post[...], pooled[...], 0, 0)).astype(BF16)
 
 
@@ -268,8 +266,7 @@
     w_key,
     w_value,
     w_out,
-    out_gain,
-    latent_out,
+    normed,
     values_t,
     keys,
     parts,
@@ -378,7 +375,7 @@
     attended = (output / total).astype(BF16)
     projected = jnp.dot(attended, w_out[...], preferred_element_type=F32)
     mean_sq = jnp.mean(projected * projected, axis=-1, keepdims=True)
-    latent_out[...] = (projected * lax.rsqrt(mean_sq + 1e-06) * out_gain[...]).astype(BF16)
+    normed[...] = projected * lax.rsqrt(mean_sq + 1e-06)
 
 
 def per_device(
@@ -410,12 +407,15 @@
     vmem = pl.BlockSpec(memory_space=pltpu.VMEM)
     hbm = pl.BlockSpec(memory_space=pl.ANY)
     dma = pltpu.SemaphoreType.DMA
-    arrived = pl.pallas_call(
+    pooled = pl.pallas_call(
         functools.partial(message_kernel, owners, n_sn, sn_blocks, targets),
-        out_shape=jax.ShapeDtypeStruct((owners, width + STAT_ROWS, BLOCK), BF16),
+        out_shape=jax.ShapeDtypeStruct((width, sn_rows), BF16),
         in_specs=[smem] * 4 + [hbm] + [vmem] * 4,
-        out_specs=pl.BlockSpec(memory_space=pl.ANY),
+        out_specs=vmem,
         scratch_shapes=[
+            pltpu.VMEM((owners, width + STAT_ROWS, BLOCK), BF16),
+            pltpu.VMEM((sn_blocks, width + STAT_ROWS, BLOCK), F32),
+            pltpu.SMEM((owners,), jnp.int32),
             pltpu.VMEM(point_features.shape[::-1], BF16),
             pltpu.VMEM((owners, 3, BLOCK), F32),
             pltpu.VMEM((owners, 3, BLOCK), F32),
@@ -443,20 +443,16 @@
         w_mid,
     )
     features_t = pl.pallas_call(
-        functools.partial(pool_kernel, owners, n_sn, sn_blocks, targets),
+        post_kernel,
         out_shape=jax.ShapeDtypeStruct((width, sn_rows), BF16),
-        in_specs=[smem] * 2 + [vmem] * 2,
+        in_specs=[vmem] * 2,
         out_specs=vmem,
-        scratch_shapes=[
-            pltpu.VMEM((sn_blocks, width + STAT_ROWS, BLOCK), F32),
-            pltpu.VMEM((width, sn_rows), BF16),
-        ],
-        name="pool",
-    )(target_block, block_slot, arrived, w_post)
-    latent_out = pl.pallas_call(
+        name="post",
+    )(pooled, w_post)
+    normed = pl.pallas_call(
         functools.partial(attend_kernel, owners, n_sn),
-        out_shape=jax.ShapeDtypeStruct((share, width), BF16),
-        in_specs=[vmem] * 6,
+        out_shape=jax.ShapeDtypeStruct((share, width), F32),
+        in_specs=[vmem] * 5,
         out_specs=vmem,
         scratch_shapes=[
             pltpu.VMEM((width, sn_rows), BF16),
@@ -469,8 +465,8 @@
         ],
         compiler_params=pltpu.CompilerParams(collective_id=1, has_side_effects=True),
         name="attend",
-    )(features_t, latent_queries.T, w_key, w_value, w_out, out_gain.reshape(1, width))
-    return (features_t.T, latent_out)
+    )(features_t, latent_queries.T, w_key, w_value, w_out)
+    return (features_t.T, (normed * out_gain).astype(BF16))
 
 
 def solution(mesh):

time: 50.1 us -> 50.9 us (1.016)
  other arithmetic: 0 us -> 1.37 us
  local copies, waits for them, and re-layouts: 1.32 us -> 0.01 us
  Pallas kernels: 47.9 us -> 48.6 us
    convert_element_type x0 -> x1, other arithmetic: none -> 1.37 us  [per_device(): return (features_t.T, (normed * out_gain).astype(BF16))]
    unnamed x1 -> x2, local copies, waits for them, and re-layouts: 1.32 us -> 0.01 us
    pallas_call x1, Pallas kernels: 3.12 us -> 2.19 us  [per_device(): pl.pallas_call(post_kernel, out_shape=jax.ShapeDtypeStruct((width, sn_row...]
    pallas_call x1, Pallas kernels: 14.8 us -> 15.7 us  [per_device(): pl.pallas_call(functools.partial(attend_kernel, owners, n_sn), out_shape=...]
    pallas_call x1, Pallas kernels: 29.9 us -> 30.7 us  [per_device(): pl.pallas_call(functools.partial(message_kernel, owners, n_sn, sn_blocks,...]
where the time goes in v3:
time: 50.9 us; the launch traced here: 50.7 us
  Pallas kernels  48.6 us (95%)
  other arithmetic  1.37 us (3%)
  between operations  0.67 us (1%)
    pallas_call x1, Pallas kernels, per_device(): pl.pallas_call(functools.partial(message_kernel, owners, n_sn, sn_blocks,...  30.7 us
    pallas_call x1, Pallas kernels, per_device(): pl.pallas_call(functools.partial(attend_kernel, owners, n_sn), out_shape=...  15.7 us
    pallas_call x1, Pallas kernels, per_device(): pl.pallas_call(post_kernel, out_shape=jax.ShapeDtypeStruct((width, sn_row...  2.19 us
    convert_element_type x1, other arithmetic, per_device(): return (features_t.T, (normed * out_gain).astype(BF16))  1.37 us

profile of v3, /device:TPU:0, one launch (start us, length us, event | category | flops | bytes accessed | tf_op | source)
XLA Modules:
  0.0 50.7 jit_solution(1067314357924033153)
XLA Ops:
  0.6 0.0 copy-start
  0.6 30.7 %messages.1.pooled = bf16[192,1024]{1,0:T(8,128)(2,1)} custom-call(s32[128]{0:T(128)} %target_block.1, s32[3,8]{1,0:T(4,128)} %bitcast.7, s32[16]{0:T(128)} %target_count.1, s32[128]{0:T(128)} %block_slot.1, bf16[192,4096]{1,0:T(8,128)(2,1)} %bitcast.5, f32[3,4096]{1,0:T(4,128)} %positions.1, f32[3,1024]{1,0:T(4,128)} %sn_positions.1, ...), custom_call_target="tpu_custom_call" | custom-call | tf_op jit(solution)/shard_map/messages/pallas_call | solution.py:410
  31.4 2.2 %post.1.features = bf16[192,1024]{1,0:T(8,128)(2,1)} custom-call(bf16[192,1024]{1,0:T(8,128)(2,1)} %messages.1.pooled, bf16[192,192]{1,0:T(8,128)(2,1)} %w_post.1), custom_call_target="tpu_custom_call" | custom-call | tf_op jit(solution)/shard_map/post/pallas_call | solution.py:445
  33.5 15.7 %attend.1 = f32[32,192]{1,0:T(8,128)} custom-call(bf16[192,1024]{1,0:T(8,128)(2,1)} %post.1.features, bf16[192,512]{1,0:T(8,128)(2,1)} %bitcast.6, bf16[192,192]{1,0:T(8,128)(2,1)} %w_key.1, bf16[192,192]{1,0:T(8,128)(2,1)} %w_value.1, bf16[192,192]{1,0:T(8,128)(2,1)} %w_out.1), custom_call_target="tpu_custom_call" | custom-call | tf_op jit(solution)/shard_map/attend/pallas_call | solution.py:452
  49.3 0.0 copy-done
  49.3 1.4 %multiply_convert_fusion = bf16[32,192]{1,0:T(8,128)(2,1)} fusion(f32[32,192]{1,0:T(8,128)} %attend.1, f32[192]{0:T(256)S(1)} %copy-done), kind=kLoop, calls=%fused_computation | loop fusion | flops 12288 | bytes 37632 | tf_op jit(solution)/shard_map/convert_element_type | solution.py:469
Async XLA Ops:
  0.6 48.6 %copy-start = (f32[192]{0:T(256)S(1)}, f32[192]{0:T(256)}, u32[]{:S(2)}) copy-start(f32[192]{0:T(256)} %param.29) | copy-start | bytes 2308

commit v4 on v3

--- a/solution.py
+++ b/solution.py
@@ -67,7 +67,14 @@
     return jnp.transpose(padded)
 
 
-def message_kernel(
+def thirds(x):
+    first = x.astype(BF16).astype(F32)
+    second = (x - first).astype(BF16).astype(F32)
+    third = x - first - second
+    return [first, second, third]
+
+
+def encoder_kernel(
     owners,
     n_sn,
     sn_blocks,
@@ -81,7 +88,20 @@
     sn_positions,
     w_in,
     w_mid,
+    w_post,
+    queries,
+    w_key,
+    w_value,
+    w_out,
+    features,
+    normed,
     pooled,
+    values_t,
+    keys,
+    parts,
+    landed,
+    part_send,
+    part_recv,
     arrived,
     sums,
     block_of,
@@ -215,23 +235,18 @@
     own_pos.wait()
     build(me)
     msg_copy(nth(owners - 2), me).start()
-    own = pltpu.make_async_copy(outgoing.at[me], arrived.at[me], own_sem.at[1])
-    own.start()
-    own.wait()
-
-    def add(source):
+    def add(source, message):
         block = block_of[source]
-        message = arrived[source].astype(F32)
         for b in range(sn_blocks):
             sums[b] += jnp.where(block == b, message, 0.0)
 
     sums[...] = jnp.zeros_like(sums)
-    add(me)
+    add(me, outgoing[me].astype(F32))
 
     def finish(i, carry):
-        copy = msg_copy(nth(owners - 2 - i), nth(owners - 2 - i))
-        copy.wait_recv()
-        add(nth(owners - 2 - i))
+        source = nth(lax.rem(i + owners // 2 + 1, owners - 1))
+        msg_copy(source, source).wait_recv()
+        add(source, arrived[source].astype(F32))
         return carry
 
     lax.fori_loop(0, owners - 1, finish, 0)
@@ -247,41 +262,12 @@
         pooled[:, b * BLOCK : (b + 1) * BLOCK] = (sums[b, :width, :] * scale).astype(BF16)
 
 
-def thirds(x):
-    first = x.astype(BF16).astype(F32)
-    second = (x - first).astype(BF16).astype(F32)
-    third = x - first - second
-    return [first, second, third]
-
-
-def post_kernel(pooled, w_post, features_out):
-    features_out[...] = jax.nn.gelu(contract(w_post[...], pooled[...], 0, 0)).astype(BF16)
-
-
-def attend_kernel(
-    owners,
-    n_sn,
-    features,
-    queries,
-    w_key,
-    w_value,
-    w_out,
-    normed,
-    values_t,
-    keys,
-    parts,
-    arrived,
-    send_sem,
-    recv_sem,
-    own_sem,
-):
-    me = place(n_sn)
-    width, latents = queries.shape
     head_width = width // HEADS
+    latents = queries.shape[1]
     share = latents // owners
     chunks = latents // LATENT_CHUNK
     per_chunk = LATENT_CHUNK // share
-    barrier = greet(owners, me, n_sn)
+    features[...] = jax.nn.gelu(contract(w_post[...], pooled[...], 0, 0)).astype(BF16)
     keys[...] = contract(features[...], w_key[...], 0, 0).astype(BF16)
     values_t[...] = contract(w_value[...], features[...], 0, 0).astype(BF16)
     row_head = lax.broadcasted_iota(jnp.int32, (width, LATENT_CHUNK), 0) // head_width
@@ -309,9 +295,9 @@
     def copy_of(other, slot_at):
         return pltpu.make_async_remote_copy(
             src_ref=parts.at[other],
-            dst_ref=arrived.at[slot_at],
-            send_sem=send_sem.at[other],
-            recv_sem=recv_sem.at[slot_at],
+            dst_ref=landed.at[slot_at],
+            send_sem=part_send.at[other],
+            recv_sem=part_recv.at[slot_at],
             device_id=peer(other, n_sn),
             device_id_type=MESH,
         )
@@ -331,7 +317,6 @@
         lax.fori_loop(0, per_chunk, start, 0)
 
     attend(0, 0)
-    pl.semaphore_wait(barrier, owners - 1)
 
     def step_on(step, carry):
         send_chunk(step - 1)
@@ -339,24 +324,24 @@
 
     lax.fori_loop(1, chunks, step_on, 0)
     send_chunk(chunks - 1)
-    own = pltpu.make_async_copy(parts.at[me], arrived.at[me], own_sem)
+    own = pltpu.make_async_copy(parts.at[me], landed.at[me], own_sem.at[1])
     own.start()
     own.wait()
 
-    def finish(off, carry):
+    def settle(off, carry):
         other = lax.rem(me + off, owners)
         copy = copy_of(other, other)
         copy.wait_send()
         copy.wait_recv()
         return carry
 
-    lax.fori_loop(1, owners, finish, 0)
+    lax.fori_loop(1, owners, settle, 0)
     lane = lax.broadcasted_iota(jnp.int32, (OUT_LANES, width), 0) - width
     head_of = lax.broadcasted_iota(jnp.int32, (OUT_LANES, width), 1) // head_width
     is_peak = jnp.logical_and(lane >= 3 * head_of, lane < 3 * head_of + 3)
     total_lane = lane - 3 * HEADS
     is_total = jnp.logical_and(total_lane >= 3 * head_of, total_lane < 3 * head_of + 3)
-    flat = jnp.concatenate([arrived[source] for source in range(owners)], axis=0)
+    flat = jnp.concatenate([landed[source] for source in range(owners)], axis=0)
     peaks = contract(flat, jnp.where(is_peak, 1.0, 0.0).astype(BF16), 1, 0)
     totals = contract(flat, jnp.where(is_total, 1.0, 0.0).astype(BF16), 1, 0)
 
@@ -370,7 +355,7 @@
     total = jnp.zeros((share, width), F32)
     for source in range(owners):
         scale = jnp.exp(of(peaks, source) - top)
-        output = output + scale * arrived[source][:, :width].astype(F32)
+        output = output + scale * landed[source][:, :width].astype(F32)
         total = total + scale * of(totals, source)
     attended = (output / total).astype(BF16)
     projected = jnp.dot(attended, w_out[...], preferred_element_type=F32)
@@ -407,12 +392,22 @@
     vmem = pl.BlockSpec(memory_space=pltpu.VMEM)
     hbm = pl.BlockSpec(memory_space=pl.ANY)
     dma = pltpu.SemaphoreType.DMA
-    pooled = pl.pallas_call(
-        functools.partial(message_kernel, owners, n_sn, sn_blocks, targets),
-        out_shape=jax.ShapeDtypeStruct((width, sn_rows), BF16),
-        in_specs=[smem] * 4 + [hbm] + [vmem] * 4,
-        out_specs=vmem,
+    features_t, normed = pl.pallas_call(
+        functools.partial(encoder_kernel, owners, n_sn, sn_blocks, targets),
+        out_shape=(
+            jax.ShapeDtypeStruct((width, sn_rows), BF16),
+            jax.ShapeDtypeStruct((share, width), F32),
+        ),
+        in_specs=[smem] * 4 + [hbm] + [vmem] * 9,
+        out_specs=(vmem, vmem),
         scratch_shapes=[
+            pltpu.VMEM((width, sn_rows), BF16),
+            pltpu.VMEM((width, sn_rows), BF16),
+            pltpu.VMEM((sn_rows, width), BF16),
+            pltpu.VMEM((owners, share, OUT_LANES), BF16),
+            pltpu.VMEM((owners, share, OUT_LANES), BF16),
+            dma((owners,)),
+            dma((owners,)),
             pltpu.VMEM((owners, width + STAT_ROWS, BLOCK), BF16),
             pltpu.VMEM((sn_blocks, width + STAT_ROWS, BLOCK), F32),
             pltpu.SMEM((owners,), jnp.int32),
@@ -430,7 +425,7 @@
             dma((3,)),
         ],
         compiler_params=pltpu.CompilerParams(collective_id=0, has_side_effects=True),
-        name="messages",
+        name="encoder",
     )(
         target_block,
         target_links.T,
@@ -441,31 +436,12 @@
         sn_positions,
         w_in,
         w_mid,
+        w_post,
+        latent_queries.T,
+        w_key,
+        w_value,
+        w_out,
     )
-    features_t = pl.pallas_call(
-        post_kernel,
-        out_shape=jax.ShapeDtypeStruct((width, sn_rows), BF16),
-        in_specs=[vmem] * 2,
-        out_specs=vmem,
-        name="post",
-    )(pooled, w_post)
-    normed = pl.pallas_call(
-        functools.partial(attend_kernel, owners, n_sn),
-        out_shape=jax.ShapeDtypeStruct((share, width), F32),
-        in_specs=[vmem] * 5,
-        out_specs=vmem,
-        scratch_shapes=[
-            pltpu.VMEM((width, sn_rows), BF16),
-            pltpu.VMEM((sn_rows, width), BF16),
-            pltpu.VMEM((owners, share, OUT_LANES), BF16),
-            pltpu.VMEM((owners, share, OUT_LANES), BF16),
-            dma((owners,)),
-            dma((owners,)),
-            dma,
-        ],
-        compiler_params=pltpu.CompilerParams(collective_id=1, has_side_effects=True),
-        name="attend",
-    )(features_t, latent_queries.T, w_key, w_value, w_out)
     return (features_t.T, (normed * out_gain).astype(BF16))
 
 

time: 50.9 us -> 46.5 us (0.914)
  Pallas kernels: 48.6 us -> 42.5 us
  local copies, waits for them, and re-layouts: 0.01 us -> 1.77 us
    pallas_call x3 -> x1, Pallas kernels: 48.6 us -> 42.5 us  [per_device(): pl.pallas_call(functools.partial(encoder_kernel, owners, n_sn, sn_blocks,...]
    unnamed x2 -> x3, local copies, waits for them, and re-layouts: 0.01 us -> 1.77 us
where the time goes in v4:
time: 46.5 us; the launch traced here: 46.3 us
  Pallas kernels  42.5 us (91%)
  local copies, waits for them, and re-layouts  1.77 us (4%)
  other arithmetic  1.37 us (3%)
  between operations  0.66 us (1%)
    pallas_call x1, Pallas kernels, per_device(): pl.pallas_call(functools.partial(encoder_kernel, owners, n_sn, sn_blocks,...  42.5 us
    unnamed x3, local copies, waits for them, and re-layouts  1.77 us
    convert_element_type x1, other arithmetic, per_device(): return (features_t.T, (normed * out_gain).astype(BF16))  1.37 us

profile of v4, /device:TPU:0, one launch (start us, length us, event | category | flops | bytes accessed | tf_op | source)
XLA Modules:
  0.0 46.3 jit_solution(18355197545754022157)
XLA Ops:
  0.6 0.0 copy-start
  0.6 42.5 %encoder.1 = (bf16[192,1024]{1,0:T(8,128)(2,1)}, f32[32,192]{1,0:T(8,128)}) custom-call(s32[128]{0:T(128)} %target_block.1, s32[3,8]{1,0:T(4,128)} %bitcast.7, s32[16]{0:T(128)} %target_count.1, s32[128]{0:T(128)} %block_slot.1, bf16[192,4096]{1,0:T(8,128)(2,1)} %bitcast.4, f32[3,4096]{1,0:T(4,128)} %positions.1, f32[3,1024]{1,0:T(4,128)} %sn_positions.1, ...), custom_call_target="tpu_custom_call" | custom-call | tf_op jit(solution)/shard_map/encoder/pallas_call | solution.py:395
  43.1 0.0 copy-done
  43.1 1.4 %multiply_convert_fusion = bf16[32,192]{1,0:T(8,128)(2,1)} fusion(f32[32,192]{1,0:T(8,128)} %get-tuple-element.5, f32[192]{0:T(256)S(1)} %copy-done), kind=kLoop, calls=%fused_computation | loop fusion | flops 12288 | bytes 37632 | tf_op jit(solution)/shard_map/convert_element_type | solution.py:445
  44.5 1.8 %copy.18 = bf16[1024,192]{0,1:T(8,128)(2,1)} copy(bf16[1024,192]{0,1:T(8,128)(2,1)} %bitcast.5) | data formatting | bytes 786432
Async XLA Ops:
  0.6 42.5 %copy-start = (f32[192]{0:T(256)S(1)}, f32[192]{0:T(256)}, u32[]{:S(2)}) copy-start(f32[192]{0:T(256)} %param.29) | copy-start | bytes 2308

commit v5 on v4

--- a/solution.py
+++ b/solution.py
@@ -12,7 +12,7 @@
 INV_RADIUS_SQ = 100.0
 MESH = pl.DeviceIdType.MESH
 STAT_ROWS = 8
-CHUNK = 512
+CHUNK = 1024
 LATENT_CHUNK = 256
 OUT_LANES = 256
 F32 = jnp.float32

time: 46.5 us -> 46.2 us (level)
  no operation moved by 1% of the time
where the time goes in v5:
time: 46.2 us; the launch traced here: 46 us
  Pallas kernels  42.2 us (91%)
  local copies, waits for them, and re-layouts  1.77 us (4%)
  other arithmetic  1.37 us (3%)
  between operations  0.66 us (1%)
    pallas_call x1, Pallas kernels, per_device(): pl.pallas_call(functools.partial(encoder_kernel, owners, n_sn, sn_blocks,...  42.2 us
    unnamed x3, local copies, waits for them, and re-layouts  1.77 us
    convert_element_type x1, other arithmetic, per_device(): return (features_t.T, (normed * out_gain).astype(BF16))  1.37 us

profile of v5, /device:TPU:0, one launch (start us, length us, event | category | flops | bytes accessed | tf_op | source)
XLA Modules:
  0.0 46.0 jit_solution(6536497702165508984)
XLA Ops:
  0.6 0.0 copy-start
  0.6 42.2 %encoder.1 = (bf16[192,1024]{1,0:T(8,128)(2,1)}, f32[32,192]{1,0:T(8,128)}) custom-call(s32[128]{0:T(128)} %target_block.1, s32[3,8]{1,0:T(4,128)} %bitcast.7, s32[16]{0:T(128)} %target_count.1, s32[128]{0:T(128)} %block_slot.1, bf16[192,4096]{1,0:T(8,128)(2,1)} %bitcast.4, f32[3,4096]{1,0:T(4,128)} %positions.1, f32[3,1024]{1,0:T(4,128)} %sn_positions.1, ...), custom_call_target="tpu_custom_call" | custom-call | tf_op jit(solution)/shard_map/encoder/pallas_call | solution.py:395
  42.8 0.0 copy-done
  42.8 1.4 %multiply_convert_fusion = bf16[32,192]{1,0:T(8,128)(2,1)} fusion(f32[32,192]{1,0:T(8,128)} %get-tuple-element.5, f32[192]{0:T(256)S(1)} %copy-done), kind=kLoop, calls=%fused_computation | loop fusion | flops 12288 | bytes 37632 | tf_op jit(solution)/shard_map/convert_element_type | solution.py:445
  44.2 1.8 %copy.18 = bf16[1024,192]{0,1:T(8,128)(2,1)} copy(bf16[1024,192]{0,1:T(8,128)(2,1)} %bitcast.5) | data formatting | bytes 786432
Async XLA Ops:
  0.6 42.2 %copy-start = (f32[192]{0:T(256)S(1)}, f32[192]{0:T(256)}, u32[]{:S(2)}) copy-start(f32[192]{0:T(256)} %param.29) | copy-start | bytes 2308
